TPU v7x, 32 devices: a whole 2x2x4 slice. The times are simulated.
32 devices in a mesh: dp: 8 (over z, y), mp: 4 (over x, core).
Axes of the slice: x: 2, y: 2, z: 4, core: 2. Of those that a mesh axis runs over, the one named last changes fastest.
Arguments:
- frames: bfloat16 [4, 4608, 768], P(None, ('dp', 'mp')), may hold values from -6 to 6
- clip_ids: int32 [4, 4608], replicated, may hold values from 0 to 5, never falling along the last dimension, each value on 1 to 1500 neighbouring positions
- w_qkv: bfloat16 [768, 3, 768], P('dp', None, 'mp'), may hold values from -0.21875 to 0.21875
- b_qv: bfloat16 [2, 4, 192], P(None, 'mp', 'dp'), may hold values from -3 to 3
- w_out: bfloat16 [768, 768], P('mp', 'dp'), may hold values from -2.5 to 2.5
- w_up: bfloat16 [768, 3072], P('dp', 'mp'), may hold values from -0.21875 to 0.21875
- b_up: bfloat16 [4, 768], P('mp', 'dp'), may hold values from -3 to 3
- w_down: bfloat16 [3072, 768], P('mp', 'dp'), may hold values from -0.109375 to 0.109375
- gains: bfloat16 [2, 768], P(None, ('dp', 'mp')), may hold values from 0.099609375 to 1.8984375
- biases: bfloat16 [4, 768], P(None, ('dp', 'mp')), may hold values from -3 to 3
- cotangent: bfloat16 [4, 4608, 768], P(None, ('dp', 'mp')), may hold values from -6 to 6
Outputs:
- output: bfloat16 [4, 4608, 768], P(None, ('dp', 'mp'))
- frames_grad: bfloat16 [4, 4608, 768], P(None, ('dp', 'mp'))
- grad_qkv: float32 [768, 3, 768], P('dp', None, 'mp')
- grad_bqv: float32 [2, 4, 192], P(None, 'mp', 'dp')
- grad_out: float32 [768, 768], P('mp', 'dp')
- grad_up: float32 [768, 3072], P('dp', 'mp')
- grad_bup: float32 [4, 768], P('mp', 'dp')
- grad_down: float32 [3072, 768], P('mp', 'dp')
- grad_gains: float32 [2, 768], P(None, ('dp', 'mp'))
- grad_biases: float32 [4, 768], P(None, ('dp', 'mp'))
Inputs may be any that keep to these rules, and one draw needn't show every extreme that they name: `clip_ids`: in each micro-batch the clip ids never fall along the frames; each clip is a run of 1 to 1500 frames, and one clip of each micro-batch has exactly 1500.
All inputs are finite; a program needn't handle non-finite values.
Results may differ from a plain program's by a relative error of at most 0.017.
Values may be sent and summed in bfloat16 or wider, within the bound.
No kernel may reach another device: no remote copies, remote signals or barrier semaphores. Data moves between devices by JAX's collectives and lax.ppermute only.
A program may use at most 192 MiB of HBM per device.

v0:
```python
import jax
import jax.numpy as jnp
from jax import lax
from jax.sharding import PartitionSpec as P

D = 768
HD = 64
CLIP = 1500
epsilon = 1e-05
masked_score = -1e30


def passed_along(array, axis, by):
    peers = lax.axis_size(axis)
    pairs = [(i, i + by) for i in range(peers) if 0 <= i + by < peers]
    return lax.ppermute(array, axis, pairs)


def shortened(array):
    return jax.tree.map(lambda a: a.astype(jnp.bfloat16) if a.dtype == jnp.float32 else a, array)


def normalize(values, gain_row, shift_row):
    middle = jnp.mean(values, axis=-1, keepdims=True)
    centred = values - middle
    spread_sq = jnp.mean(centred * centred, axis=-1, keepdims=True)
    return centred * lax.rsqrt(spread_sq + epsilon) * gain_row + shift_row


def gelu_exact(values):
    return jax.nn.gelu(values, approximate=False)


def fetch_weights(w_qkv, b_qv, w_out, w_up, b_up, w_down, gains, biases):
    gathered = (
        lax.all_gather(w_qkv, "dp", axis=0, tiled=True),
        lax.all_gather(b_qv, "dp", axis=2, tiled=True),
        lax.all_gather(w_out, "dp", axis=1, tiled=True),
        lax.all_gather(w_up, "dp", axis=0, tiled=True),
        lax.all_gather(b_up, "dp", axis=1, tiled=True),
        lax.all_gather(w_down, "dp", axis=1, tiled=True),
    )
    norm_rows = (
        lax.all_gather(gains, ("dp", "mp"), axis=1, tiled=True),
        lax.all_gather(biases, ("dp", "mp"), axis=1, tiled=True),
    )
    return (gathered, norm_rows)


def spread_rows(values):
    return lax.all_gather(values, "mp", axis=0, tiled=True)


def spread_grads(values):
    return lax.all_gather(values, "mp", axis=0, tiled=True)


def project_sum(left, weight, share_rows):

    def term(row_start, row_count):
        row_piece = lax.dynamic_slice_in_dim(left, row_start, row_count, 0)
        return jnp.dot(row_piece, weight, preferred_element_type=jnp.float32)

    return lax.psum_scatter(
        term(jnp.int32(0), share_rows * lax.axis_size("mp")).astype(jnp.bfloat16),
        "mp",
        scatter_dimension=0,
        tiled=True,
    ).astype(jnp.float32)


def project_back(left, weight, share_rows):

    def term(row_start, row_count):
        row_piece = lax.dynamic_slice_in_dim(left, row_start, row_count, 0)
        return lax.dot_general(
            row_piece, weight, (((1,), (1,)), ((), ())), preferred_element_type=jnp.float32
        )

    return lax.psum_scatter(
        term(jnp.int32(0), share_rows * lax.axis_size("mp")).astype(jnp.bfloat16),
        "mp",
        scatter_dimension=0,
        tiled=True,
    ).astype(jnp.float32)


def head_scores(query_head, key_head, same_clip):
    scores = jnp.einsum(
        "qd,kd->qk", query_head, key_head, preferred_element_type=jnp.float32
    ) * HD ** (-0.5)
    return jnp.where(same_clip, scores, masked_score)


def local(frames, clip_ids, w_qkv, b_qv, w_out, w_up, b_up, w_down, gains, biases, cotangent):
    share_rows = frames.shape[1]
    row_total = share_rows * lax.axis_size("mp")
    device = lax.axis_index("dp")
    frame_total = clip_ids.shape[1]
    width_local = w_qkv.shape[2]
    ff_local = w_up.shape[1]
    heads_local = width_local // HD
    reach_devs = (CLIP + row_total - 2) // row_total
    offsets = list(range(-reach_devs, reach_devs + 1))
    window = len(offsets) * row_total
    score_scale = HD ** (-0.5)
    key_place = (device - reach_devs) * row_total + jnp.arange(window, dtype=jnp.int32)
    key_valid = (key_place >= 0) & (key_place < frame_total)
    key_index = jnp.clip(key_place, 0, frame_total - 1)
    query_index = device * row_total + jnp.arange(row_total, dtype=jnp.int32)

    def forward_pass(inputs, clip_row, fetched):
        weights, norm_rows = fetched
        weight_qkv, bias_qv, weight_out, weight_up, bias_up, weight_down = weights
        gain_rows = norm_rows[0].astype(jnp.float32)
        bias_rows = norm_rows[1].astype(jnp.float32)
        key_clip = jnp.where(key_valid, jnp.take(clip_row, key_index), -1)
        query_clip = jnp.take(clip_row, query_index)
        same_clip = query_clip[:, None] == key_clip[None, :]
        resid_in = inputs.astype(jnp.float32)
        normed_one = normalize(resid_in, gain_rows[0], bias_rows[0]).astype(jnp.bfloat16)
        rows_one = spread_rows(normed_one)
        projected = jnp.dot(
            rows_one,
            weight_qkv.reshape(weight_qkv.shape[0], -1),
            preferred_element_type=jnp.float32,
        ).reshape(row_total, 3, width_local)
        bias_pair = bias_qv.reshape(2, width_local).astype(jnp.float32)
        projected = (
            projected + jnp.stack([bias_pair[0], jnp.zeros_like(bias_pair[0]), bias_pair[1]])[None]
        )
        projected = projected.astype(jnp.bfloat16)
        queries = projected[:, 0]
        key_value = projected[:, 1:]
        pieces = []
        for offset in offsets:
            if offset == 0:
                pieces.append(key_value)
            else:
                pieces.append(passed_along(key_value, "dp", -offset))
        near_rows = jnp.concatenate(pieces, axis=0)
        keys_near = near_rows[:, 0]
        values_near = near_rows[:, 1]
        head_outs = []
        log_totals = []
        for head_index in range(heads_local):
            columns = slice(head_index * HD, (head_index + 1) * HD)
            scores = head_scores(queries[:, columns], keys_near[:, columns], same_clip)
            top_score = jnp.max(scores, axis=-1, keepdims=True)
            log_total = top_score + jnp.log(
                jnp.sum(jnp.exp(scores - top_score), axis=-1, keepdims=True)
            )
            soft_weights = jnp.exp(scores - log_total).astype(jnp.bfloat16)
            head_outs.append(
                jnp.dot(soft_weights, values_near[:, columns], preferred_element_type=jnp.float32)
            )
            log_totals.append(log_total)
        attended = jnp.concatenate(head_outs, axis=-1).astype(jnp.bfloat16)
        mixed_rows = resid_in + project_sum(attended, weight_out, share_rows) + bias_rows[1]
        normed_two = normalize(mixed_rows, gain_rows[1], bias_rows[2]).astype(jnp.bfloat16)
        rows_two = spread_rows(normed_two)
        hidden = jnp.dot(rows_two, weight_up, preferred_element_type=jnp.float32) + bias_up.reshape(
            -1
        ).astype(jnp.float32)
        activated = gelu_exact(hidden).astype(jnp.bfloat16)
        result = mixed_rows + project_sum(activated, weight_down, share_rows) + bias_rows[3]
        kept_state = (
            resid_in,
            rows_one,
            queries,
            keys_near,
            values_near,
            same_clip,
            log_totals,
            attended,
            mixed_rows,
            rows_two,
            hidden,
            activated,
            query_clip,
            clip_row,
        )
        return (kept_state, result)

    def backward_pass(kept_state, cot_rows, fetched):
        weights, norm_rows = fetched
        weight_qkv, bias_qv, weight_out, weight_up, bias_up, weight_down = weights
        gain_rows = norm_rows[0].astype(jnp.float32)
        bias_rows = norm_rows[1].astype(jnp.float32)
        (
            resid_in,
            rows_one,
            queries,
            keys_near,
            values_near,
            same_clip,
            log_totals,
            attended,
            mixed_rows,
            rows_two,
            hidden,
            activated,
            query_clip,
            clip_row,
        ) = kept_state
        grad_result = cot_rows.astype(jnp.float32)
        rows_result = spread_grads(grad_result.astype(jnp.bfloat16))
        grad_wdown = jnp.einsum(
            "nf,nd->fd", activated, rows_result, preferred_element_type=jnp.float32
        )
        grad_act = lax.dot_general(
            rows_result, weight_down, (((1,), (1,)), ((), ())), preferred_element_type=jnp.float32
        )
        gelu_pull = jax.vjp(gelu_exact, hidden)[1]
        grad_hidden = gelu_pull(grad_act)[0].astype(jnp.bfloat16)
        grad_wup = jnp.einsum(
            "nd,nf->df", rows_two, grad_hidden, preferred_element_type=jnp.float32
        )
        grad_bup = jnp.sum(grad_hidden, axis=0, dtype=jnp.float32).reshape(1, ff_local)
        grad_two = project_back(grad_hidden, weight_up, share_rows)
        norm_pull_two = jax.vjp(normalize, mixed_rows, gain_rows[1], bias_rows[2])[1]
        grad_mix, grad_gain_two, grad_bias_two = norm_pull_two(grad_two)
        grad_mixed = grad_result + grad_mix
        rows_mixed = spread_grads(grad_mixed.astype(jnp.bfloat16))
        grad_wout = jnp.einsum(
            "nh,nd->hd", attended, rows_mixed, preferred_element_type=jnp.float32
        )
        grad_att = lax.dot_general(
            rows_mixed, weight_out, (((1,), (1,)), ((), ())), preferred_element_type=jnp.float32
        ).astype(jnp.bfloat16)
        query_grads = []
        key_grads = []
        value_grads = []
        row_deltas = []
        for head_index in range(heads_local):
            columns = slice(head_index * HD, (head_index + 1) * HD)
            query_head = queries[:, columns]
            key_head = keys_near[:, columns]
            grad_head = grad_att[:, columns]
            scores = head_scores(query_head, key_head, same_clip)
            soft_weights = jnp.exp(scores - log_totals[head_index])
            grad_soft = jnp.einsum(
                "qd,kd->qk", grad_head, values_near[:, columns], preferred_element_type=jnp.float32
            )
            row_delta = jnp.sum(grad_soft * soft_weights, axis=-1, keepdims=True)
            row_deltas.append(row_delta)
            grad_scores = (soft_weights * (grad_soft - row_delta)).astype(jnp.bfloat16)
            query_grads.append(
                jnp.dot(grad_scores, key_head, preferred_element_type=jnp.float32) * score_scale
            )
            key_grads.append(
                jnp.einsum("qk,qd->kd", grad_scores, query_head, preferred_element_type=jnp.float32)
                * score_scale
            )
            value_grads.append(
                jnp.einsum(
                    "qk,qd->kd",
                    soft_weights.astype(jnp.bfloat16),
                    grad_head,
                    preferred_element_type=jnp.float32,
                )
            )
        grad_queries = jnp.concatenate(query_grads, axis=-1)
        kv_total = jnp.zeros((row_total, 2, width_local), jnp.float32)
        stacked = jnp.stack(
            [jnp.concatenate(key_grads, axis=-1), jnp.concatenate(value_grads, axis=-1)], axis=1
        )
        for place_index, offset in enumerate(offsets):
            segment_grad = stacked[place_index * row_total : (place_index + 1) * row_total]
            if offset == 0:
                kv_total = kv_total + segment_grad
            else:
                kv_total = kv_total + passed_along(shortened(segment_grad), "dp", offset).astype(
                    segment_grad.dtype
                )
        grad_proj = jnp.concatenate([grad_queries[:, None], kv_total], axis=1).astype(jnp.bfloat16)
        grad_wqkv = jnp.einsum(
            "nd,nce->dce", rows_one, grad_proj, preferred_element_type=jnp.float32
        )
        grad_bqv = jnp.stack(
            [
                jnp.sum(grad_proj[:, 0], axis=0, dtype=jnp.float32),
                jnp.sum(grad_proj[:, 2], axis=0, dtype=jnp.float32),
            ]
        ).reshape(2, 1, width_local)
        grad_one = project_back(
            grad_proj.reshape(row_total, -1),
            weight_qkv.reshape(weight_qkv.shape[0], -1),
            share_rows,
        )
        norm_pull_one = jax.vjp(normalize, resid_in, gain_rows[0], bias_rows[0])[1]
        grad_in_norm, grad_gain_one, grad_bias_one = norm_pull_one(grad_one)
        grad_inputs = (grad_mixed + grad_in_norm).astype(jnp.bfloat16)
        grad_gain_rows = jnp.stack([grad_gain_one, grad_gain_two])
        grad_bias_rows = jnp.stack(
            [
                grad_bias_one,
                jnp.sum(grad_mixed, axis=0),
                grad_bias_two,
                jnp.sum(grad_result, axis=0),
            ]
        )
        grad_parts = (
            grad_wqkv,
            grad_bqv,
            grad_wout,
            grad_wup,
            grad_bup,
            grad_wdown,
            grad_gain_rows,
            grad_bias_rows,
        )
        return (grad_parts, grad_inputs)

    def step(totals, step_items):
        inputs, clip_row, cot_rows = step_items
        front_weights = fetch_weights(w_qkv, b_qv, w_out, w_up, b_up, w_down, gains, biases)
        kept_state, result = forward_pass(inputs, clip_row, front_weights)
        fenced = lax.optimization_barrier(
            (w_qkv, b_qv, w_out, w_up, b_up, w_down, gains, biases, result)
        )
        behind = fetch_weights(
            fenced[0], fenced[1], fenced[2], fenced[3], fenced[4], fenced[5], fenced[6], fenced[7]
        )
        grad_parts, grad_inputs = backward_pass(kept_state, cot_rows, behind)
        totals = tuple((running + grad_part for running, grad_part in zip(totals, grad_parts)))
        return (totals, (result.astype(jnp.bfloat16), grad_inputs))

    zeros_start = (
        jnp.zeros((D, 3, width_local), jnp.float32),
        jnp.zeros((2, 1, width_local), jnp.float32),
        jnp.zeros((width_local, D), jnp.float32),
        jnp.zeros((D, ff_local), jnp.float32),
        jnp.zeros((1, ff_local), jnp.float32),
        jnp.zeros((ff_local, D), jnp.float32),
        jnp.zeros((2, D), jnp.float32),
        jnp.zeros((4, D), jnp.float32),
    )
    totals, (output, frames_grad) = lax.scan(step, zeros_start, (frames, clip_ids, cotangent))
    owned = (
        lax.psum_scatter(totals[0], "dp", scatter_dimension=0, tiled=True),
        lax.psum_scatter(totals[1], "dp", scatter_dimension=2, tiled=True),
        lax.psum_scatter(totals[2], "dp", scatter_dimension=1, tiled=True),
        lax.psum_scatter(totals[3], "dp", scatter_dimension=0, tiled=True),
        lax.psum_scatter(totals[4], "dp", scatter_dimension=1, tiled=True),
        lax.psum_scatter(totals[5], "dp", scatter_dimension=1, tiled=True),
    )
    owned_norms = (
        lax.psum_scatter(totals[6], ("dp", "mp"), scatter_dimension=1, tiled=True),
        lax.psum_scatter(totals[7], ("dp", "mp"), scatter_dimension=1, tiled=True),
    )
    return (
        output,
        frames_grad,
        owned[0],
        owned[1],
        owned[2],
        owned[3],
        owned[4],
        owned[5],
        owned_norms[0],
        owned_norms[1],
    )


def solution(mesh):
    placed = (
        P(None, ("dp", "mp"), None),
        P(),
        P("dp", None, "mp"),
        P(None, "mp", "dp"),
        P("mp", "dp"),
        P("dp", "mp"),
        P("mp", "dp"),
        P("mp", "dp"),
        P(None, ("dp", "mp")),
        P(None, ("dp", "mp")),
        P(None, ("dp", "mp"), None),
    )
    return jax.shard_map(
        local,
        mesh=mesh,
        in_specs=placed,
        out_specs=(
            P(None, ("dp", "mp"), None),
            P(None, ("dp", "mp"), None),
            P("dp", None, "mp"),
            P(None, "mp", "dp"),
            P("mp", "dp"),
            P("dp", "mp"),
            P("mp", "dp"),
            P("mp", "dp"),
            P(None, ("dp", "mp")),
            P(None, ("dp", "mp")),
        ),
        check_vma=False,
    )
```

profile of v0, /device:TPU:0, one launch (start us, length us, event | category | flops | bytes accessed | tf_op | source)
XLA Modules:
  0.0 3567.8 jit_solution(23908522268389208)
XLA Ops:
  9.8 3200.0 %while.31 = (s32[]{:T(128)}, f32[768,3,192]{0,2,1:T(8,128)}, f32[2,1,192]{2,1,0:T(1,128)}, f32[192,768]{1,0:T(8,128)}, f32[768,768]{1,0:T(8,128)}, /*index=5*/f3...) while((s32[]{:T(128)}, f32[768,3,192]{0,2,1:T(8,128)}, ...), condition=%wide.region_31.32_spmd.clone.clone.clone, body=%wide.region_0.31_spmd.clone.clone.clone.sunk | while | flops 11638805504 | bytes 781726784 | solution.py:339
  12.4 43.5 %all-gather.21 = bf16[32,24,2]{1,2,0:T(2,128)(2,1)S(1)} all-gather(bf16[1,24,2]{1,2,0:T(2,128)(2,1)} %bitcast.337), channel_id=1, replica_groups=mesh['dp'=8,'mp'=4] {'dp','mp'}, dimensions={0}, use_global_device_ids=true | all-gather | bytes 3168 | tf_op jit(solution)/shard_map/while/body/eval_jaxpr/all_gather | solution.py:44
  56.1 37.0 %all-gather.20 = bf16[32,24,4]{1,2,0:T(4,128)(2,1)S(1)} all-gather(bf16[1,24,4]{1,2,0:T(4,128)(2,1)} %bitcast.340), channel_id=1, replica_groups=mesh['dp'=8,'mp'=4] {'dp','mp'}, dimensions={0}, use_global_device_ids=true | all-gather | bytes 6336 | tf_op jit(solution)/shard_map/while/body/eval_jaxpr/all_gather | solution.py:45
  93.4 30.6 all_gather.101
  136.7 37.0 %all_gather.99 = bf16[768,3,192]{2,1,0:T(4,128)(2,1)S(1)} all-gather(bf16[96,3,192]{2,1,0:T(4,128)(2,1)S(1)} %copy.86), channel_id=1, replica_groups=mesh['dp'=8,'mp'=4] {'dp'}, dimensions={0}, use_global_device_ids=true | all-gather | bytes 995328 | tf_op jit(solution)/shard_map/while/body/eval_jaxpr/all_gather | solution.py:36
  194.2 22.7 gather_fusion
  216.9 33.2 all_gather.102
  314.0 23.7 all-reduce.9
  368.2 34.0 all-gather.31.cloned.1.call-done
  405.7 22.3 reduce-scatter.29.cloned.1.call-done
  440.5 30.7 all-gather.33.cloned.1.call-done
  476.7 36.6 %all-gather.35.cloned.1.call-done = bf16[768,768]{1,0:T(8,128)(2,1)} async-done(((bf16[96,768]{1,0:T(8,128)(2,1)}), bf16[768,768]{1,0:T(8,128)(2,1)}) %all-gather.35.cloned.1.call-update) | async-done | bytes 1179664 | tf_op jit(solution)/shard_map/while/body/eval_jaxpr/all_gather | solution.py:39
  521.3 38.9 %all-gather.23 = bf16[32,24,2]{1,2,0:T(2,128)(2,1)S(1)} all-gather(bf16[1,24,2]{1,2,0:T(2,128)(2,1)S(1)} %bitcast.338), channel_id=1, replica_groups=mesh['dp'=8,'mp'=4] {'dp','mp'}, dimensions={0}, use_global_device_ids=true | all-gather | bytes 3168 | tf_op jit(solution)/shard_map/while/body/eval_jaxpr/all_gather | solution.py:44
  560.5 33.6 all_gather.109
  594.1 37.0 %all_gather.110 = bf16[768,3,192]{2,0,1:T(8,128)(2,1)} all-gather(bf16[96,3,192]{2,0,1:T(8,128)(2,1)S(1)} %copy-done.32), channel_id=1, replica_groups=mesh['dp'=8,'mp'=4] {'dp'}, dimensions={0}, use_global_device_ids=true | all-gather | bytes 995328 | tf_op jit(solution)/shard_map/while/body/eval_jaxpr/all_gather | solution.py:36
  769.8 35.0 reduce-scatter.33.cloned.1.call-done
  812.0 40.7 %all-gather.21 = bf16[32,24,2]{1,2,0:T(2,128)(2,1)S(1)} all-gather(bf16[1,24,2]{1,2,0:T(2,128)(2,1)} %bitcast.337), channel_id=1, replica_groups=mesh['dp'=8,'mp'=4] {'dp','mp'}, dimensions={0}, use_global_device_ids=true | all-gather | bytes 3168 | tf_op jit(solution)/shard_map/while/body/eval_jaxpr/all_gather | solution.py:44
  853.0 37.0 %all-gather.20 = bf16[32,24,4]{1,2,0:T(4,128)(2,1)S(1)} all-gather(bf16[1,24,4]{1,2,0:T(4,128)(2,1)} %bitcast.340), channel_id=1, replica_groups=mesh['dp'=8,'mp'=4] {'dp','mp'}, dimensions={0}, use_global_device_ids=true | all-gather | bytes 6336 | tf_op jit(solution)/shard_map/while/body/eval_jaxpr/all_gather | solution.py:45
  890.3 30.6 all_gather.101
  933.5 37.0 %all_gather.99 = bf16[768,3,192]{2,1,0:T(4,128)(2,1)S(1)} all-gather(bf16[96,3,192]{2,1,0:T(4,128)(2,1)S(1)} %copy.86), channel_id=1, replica_groups=mesh['dp'=8,'mp'=4] {'dp'}, dimensions={0}, use_global_device_ids=true | all-gather | bytes 995328 | tf_op jit(solution)/shard_map/while/body/eval_jaxpr/all_gather | solution.py:36
  991.0 22.7 gather_fusion
  1013.8 33.2 all_gather.102
  1110.7 23.7 all-reduce.9
  1165.0 34.3 all-gather.31.cloned.1.call-done
  1237.4 30.9 all-gather.33.cloned.1.call-done
  1273.7 36.4 %all-gather.35.cloned.1.call-done = bf16[768,768]{1,0:T(8,128)(2,1)} async-done(((bf16[96,768]{1,0:T(8,128)(2,1)}), bf16[768,768]{1,0:T(8,128)(2,1)}) %all-gather.35.cloned.1.call-update) | async-done | bytes 1179664 | tf_op jit(solution)/shard_map/while/body/eval_jaxpr/all_gather | solution.py:39
  1318.9 38.9 %all-gather.23 = bf16[32,24,2]{1,2,0:T(2,128)(2,1)S(1)} all-gather(bf16[1,24,2]{1,2,0:T(2,128)(2,1)S(1)} %bitcast.338), channel_id=1, replica_groups=mesh['dp'=8,'mp'=4] {'dp','mp'}, dimensions={0}, use_global_device_ids=true | all-gather | bytes 3168 | tf_op jit(solution)/shard_map/while/body/eval_jaxpr/all_gather | solution.py:44
  1358.1 33.6 all_gather.109
  1391.7 37.0 %all_gather.110 = bf16[768,3,192]{2,0,1:T(8,128)(2,1)} all-gather(bf16[96,3,192]{2,0,1:T(8,128)(2,1)S(1)} %copy-done.32), channel_id=1, replica_groups=mesh['dp'=8,'mp'=4] {'dp'}, dimensions={0}, use_global_device_ids=true | all-gather | bytes 995328 | tf_op jit(solution)/shard_map/while/body/eval_jaxpr/all_gather | solution.py:36
  1570.9 33.2 reduce-scatter.33.cloned.1.call-done
  1611.3 40.7 %all-gather.21 = bf16[32,24,2]{1,2,0:T(2,128)(2,1)S(1)} all-gather(bf16[1,24,2]{1,2,0:T(2,128)(2,1)} %bitcast.337), channel_id=1, replica_groups=mesh['dp'=8,'mp'=4] {'dp','mp'}, dimensions={0}, use_global_device_ids=true | all-gather | bytes 3168 | tf_op jit(solution)/shard_map/while/body/eval_jaxpr/all_gather | solution.py:44
  1652.4 37.0 %all-gather.20 = bf16[32,24,4]{1,2,0:T(4,128)(2,1)S(1)} all-gather(bf16[1,24,4]{1,2,0:T(4,128)(2,1)} %bitcast.340), channel_id=1, replica_groups=mesh['dp'=8,'mp'=4] {'dp','mp'}, dimensions={0}, use_global_device_ids=true | all-gather | bytes 6336 | tf_op jit(solution)/shard_map/while/body/eval_jaxpr/all_gather | solution.py:45
  1689.7 30.6 all_gather.101
  1732.9 37.0 %all_gather.99 = bf16[768,3,192]{2,1,0:T(4,128)(2,1)S(1)} all-gather(bf16[96,3,192]{2,1,0:T(4,128)(2,1)S(1)} %copy.86), channel_id=1, replica_groups=mesh['dp'=8,'mp'=4] {'dp'}, dimensions={0}, use_global_device_ids=true | all-gather | bytes 995328 | tf_op jit(solution)/shard_map/while/body/eval_jaxpr/all_gather | solution.py:36
  1790.4 22.7 gather_fusion
  1813.1 33.2 all_gather.102
  1909.9 23.8 all-reduce.9
  1964.2 34.1 all-gather.31.cloned.1.call-done
  2036.6 30.7 all-gather.33.cloned.1.call-done
  2072.8 36.6 %all-gather.35.cloned.1.call-done = bf16[768,768]{1,0:T(8,128)(2,1)} async-done(((bf16[96,768]{1,0:T(8,128)(2,1)}), bf16[768,768]{1,0:T(8,128)(2,1)}) %all-gather.35.cloned.1.call-update) | async-done | bytes 1179664 | tf_op jit(solution)/shard_map/while/body/eval_jaxpr/all_gather | solution.py:39
  2118.2 38.9 %all-gather.23 = bf16[32,24,2]{1,2,0:T(2,128)(2,1)S(1)} all-gather(bf16[1,24,2]{1,2,0:T(2,128)(2,1)S(1)} %bitcast.338), channel_id=1, replica_groups=mesh['dp'=8,'mp'=4] {'dp','mp'}, dimensions={0}, use_global_device_ids=true | all-gather | bytes 3168 | tf_op jit(solution)/shard_map/while/body/eval_jaxpr/all_gather | solution.py:44
  2157.4 33.6 all_gather.109
  2191.0 37.0 %all_gather.110 = bf16[768,3,192]{2,0,1:T(8,128)(2,1)} all-gather(bf16[96,3,192]{2,0,1:T(8,128)(2,1)S(1)} %copy-done.32), channel_id=1, replica_groups=mesh['dp'=8,'mp'=4] {'dp'}, dimensions={0}, use_global_device_ids=true | all-gather | bytes 995328 | tf_op jit(solution)/shard_map/while/body/eval_jaxpr/all_gather | solution.py:36
  2370.2 33.2 reduce-scatter.33.cloned.1.call-done
  2410.6 40.7 %all-gather.21 = bf16[32,24,2]{1,2,0:T(2,128)(2,1)S(1)} all-gather(bf16[1,24,2]{1,2,0:T(2,128)(2,1)} %bitcast.337), channel_id=1, replica_groups=mesh['dp'=8,'mp'=4] {'dp','mp'}, dimensions={0}, use_global_device_ids=true | all-gather | bytes 3168 | tf_op jit(solution)/shard_map/while/body/eval_jaxpr/all_gather | solution.py:44
  2451.6 37.0 %all-gather.20 = bf16[32,24,4]{1,2,0:T(4,128)(2,1)S(1)} all-gather(bf16[1,24,4]{1,2,0:T(4,128)(2,1)} %bitcast.340), channel_id=1, replica_groups=mesh['dp'=8,'mp'=4] {'dp','mp'}, dimensions={0}, use_global_device_ids=true | all-gather | bytes 6336 | tf_op jit(solution)/shard_map/while/body/eval_jaxpr/all_gather | solution.py:45
  2488.9 30.6 all_gather.101
  2532.2 37.0 %all_gather.99 = bf16[768,3,192]{2,1,0:T(4,128)(2,1)S(1)} all-gather(bf16[96,3,192]{2,1,0:T(4,128)(2,1)S(1)} %copy.86), channel_id=1, replica_groups=mesh['dp'=8,'mp'=4] {'dp'}, dimensions={0}, use_global_device_ids=true | all-gather | bytes 995328 | tf_op jit(solution)/shard_map/while/body/eval_jaxpr/all_gather | solution.py:36
  2589.7 22.7 gather_fusion
  2612.4 33.2 all_gather.102
  2709.2 23.8 all-reduce.9
  2763.4 34.1 all-gather.31.cloned.1.call-done
  2801.0 22.3 reduce-scatter.29.cloned.1.call-done
  2835.8 30.7 all-gather.33.cloned.1.call-done
  2872.0 36.6 %all-gather.35.cloned.1.call-done = bf16[768,768]{1,0:T(8,128)(2,1)} async-done(((bf16[96,768]{1,0:T(8,128)(2,1)}), bf16[768,768]{1,0:T(8,128)(2,1)}) %all-gather.35.cloned.1.call-update) | async-done | bytes 1179664 | tf_op jit(solution)/shard_map/while/body/eval_jaxpr/all_gather | solution.py:39
  2917.4 38.9 %all-gather.23 = bf16[32,24,2]{1,2,0:T(2,128)(2,1)S(1)} all-gather(bf16[1,24,2]{1,2,0:T(2,128)(2,1)S(1)} %bitcast.338), channel_id=1, replica_groups=mesh['dp'=8,'mp'=4] {'dp','mp'}, dimensions={0}, use_global_device_ids=true | all-gather | bytes 3168 | tf_op jit(solution)/shard_map/while/body/eval_jaxpr/all_gather | solution.py:44
  2956.6 33.6 all_gather.109
  2990.2 37.0 %all_gather.110 = bf16[768,3,192]{2,0,1:T(8,128)(2,1)} all-gather(bf16[96,3,192]{2,0,1:T(8,128)(2,1)S(1)} %copy-done.32), channel_id=1, replica_groups=mesh['dp'=8,'mp'=4] {'dp'}, dimensions={0}, use_global_device_ids=true | all-gather | bytes 995328 | tf_op jit(solution)/shard_map/while/body/eval_jaxpr/all_gather | solution.py:36
  3169.3 33.2 reduce-scatter.33.cloned.1.call-done
  3243.7 37.3 %all-reduce.7 = (f32[2,768]{1,0:T(2,128)S(1)}, f32[4,768]{1,0:T(4,128)S(1)}) all-reduce(f32[2,768]{1,0:T(2,128)S(1)} %copy-done.55, f32[4,768]{1,0:T(4,128)S(1)} %copy-done.42), channel_id=13, replica_groups=mesh['dp'=8,'mp'=4] {'dp','mp'}, use_global_device_ids=true, to_apply=%region_38.39.clone | all-reduce | flops 4608 | bytes 36864
  3284.4 56.9 %reduce-scatter.23.cloned.1.call-done = f32[96,192]{1,0:T(8,128)} async-done(((f32[768,192]{1,0:T(8,128)}), f32[96,192]{1,0:T(8,128)}) %reduce-scatter.23.cloned.1.call-update) | async-done | bytes 73744
  3342.9 71.2 %reduce-scatter.17.cloned.1.call-done = f32[96,3,192]{2,0,1:T(8,128)} async-done(((f32[768,3,192]{2,0,1:T(8,128)}), f32[96,3,192]{2,0,1:T(8,128)}) %reduce-scatter.17.cloned.1.call-update) | async-done | bytes 221200 | tf_op jit(solution)/shard_map/reduce_scatter | solution.py:341
  3414.1 72.8 %reduce-scatter.19.cloned.1.call-done = f32[96,768]{1,0:T(8,128)} async-done(((f32[768,768]{1,0:T(8,128)}), f32[96,768]{1,0:T(8,128)}) %reduce-scatter.19.cloned.1.call-update) | async-done | bytes 294928 | tf_op jit(solution)/shard_map/reduce_scatter | solution.py:344
  3486.8 73.1 %reduce-scatter.21.cloned.1.call-done = f32[768,96]{0,1:T(8,128)} async-done(((f32[768,768]{0,1:T(8,128)}), f32[768,96]{0,1:T(8,128)}) %reduce-scatter.21.cloned.1.call-update) | async-done | bytes 294928 | tf_op jit(solution)/shard_map/reduce_scatter | solution.py:346
  (1362 shorter events, 1301.9 us)
Async XLA Ops:
  10.1 330.3 %reduce-scatter.27.cloned.1.call-start = ((), (), s32[]{:S(2)}) async-start(), calls=%async_computation.14 | async-start | bytes 1105920 | tf_op jit(solution)/shard_map/while/body/eval_jaxpr/reduce_scatter | solution.py:64
  175.7 74.5 %collective-permute-start.5 = (bf16[576,2,192]{0,2,1:T(8,128)(2,1)S(1)}, bf16[576,2,192]{0,2,1:T(8,128)(2,1)S(1)}, u32[]{:S(2)}, u32[]{:S(2)}) collective-permute-start(bf16[576,2,192]{0,2,1:T(8,128)(2,1)S(1)} %slice.463), channel_id=1, source_target_pairs={{12,0},{16,4},{20,8},{24,12},{28,16},{13,1},{17,5},{21,9},{25,13},... | collective-permute-start | bytes 1327112 | tf_op jit(solution)/shard_map/while/body/eval_jaxpr/ppermute | solution.py:16
  177.0 77.0 %collective-permute-start.4 = (bf16[576,2,192]{0,2,1:T(8,128)(2,1)S(1)}, bf16[576,2,192]{0,2,1:T(8,128)(2,1)S(1)}, u32[]{:S(2)}, u32[]{:S(2)}) collective-permute-start(bf16[576,2,192]{0,2,1:T(8,128)(2,1)S(1)} %slice.463), channel_id=1, source_target_pairs={{8,0},{12,4},{16,8},{20,12},{24,16},{28,20},{9,1},{13,5},{17,9},{2... | collective-permute-start | bytes 1327112 | tf_op jit(solution)/shard_map/while/body/eval_jaxpr/ppermute | solution.py:16
  178.3 75.7 %collective-permute-start.3 = (bf16[576,2,192]{0,2,1:T(8,128)(2,1)S(1)}, bf16[576,2,192]{0,2,1:T(8,128)(2,1)S(1)}, u32[]{:S(2)}, u32[]{:S(2)}) collective-permute-start(bf16[576,2,192]{0,2,1:T(8,128)(2,1)S(1)} %slice.463), channel_id=1, source_target_pairs={{4,0},{8,4},{12,8},{16,12},{20,16},{24,20},{28,24},{5,1},{9,5},{13... | collective-permute-start | bytes 1327112 | tf_op jit(solution)/shard_map/while/body/eval_jaxpr/ppermute | solution.py:16
  179.6 74.4 %collective-permute-start.2 = (bf16[576,2,192]{0,2,1:T(8,128)(2,1)S(1)}, bf16[576,2,192]{0,2,1:T(8,128)(2,1)}, u32[]{:S(2)}, u32[]{:S(2)}) collective-permute-start(bf16[576,2,192]{0,2,1:T(8,128)(2,1)S(1)} %slice.463), channel_id=1, source_target_pairs={{0,4},{4,8},{8,12},{12,16},{16,20},{20,24},{24,28},{1,5},{5,9},{9,... | collective-permute-start | bytes 1327112 | tf_op jit(solution)/shard_map/while/body/eval_jaxpr/ppermute | solution.py:16
  184.9 69.1 %collective-permute-start.1 = (bf16[576,2,192]{0,2,1:T(8,128)(2,1)S(1)}, bf16[576,2,192]{0,2,1:T(8,128)(2,1)}, u32[]{:S(2)}, u32[]{:S(2)}) collective-permute-start(bf16[576,2,192]{0,2,1:T(8,128)(2,1)S(1)} %slice.463), channel_id=1, source_target_pairs={{0,8},{4,12},{8,16},{12,20},{16,24},{20,28},{1,9},{5,13},{9,17},{1... | collective-permute-start | bytes 1327112 | tf_op jit(solution)/shard_map/while/body/eval_jaxpr/ppermute | solution.py:16
  311.2 49.1 %all-gather.29.cloned.1.call-start = ((), (), s32[]{:S(2)}) async-start(), calls=%async_computation.15 | async-start | bytes 1327104 | tf_op jit(solution)/shard_map/while/body/eval_jaxpr/all_gather | solution.py:39
  311.8 90.4 %all-gather.31.cloned.1.call-start = ((), (), s32[]{:S(2)}) async-start(), calls=%async_computation.16 | async-start | bytes 1327104 | tf_op jit(solution)/shard_map/while/body/eval_jaxpr/all_gather | solution.py:41
  312.4 115.5 %reduce-scatter.29.cloned.1.call-start = ((), (), s32[]{:S(2)}) async-start(), calls=%async_computation.17 | async-start | bytes 1105920 | tf_op jit(solution)/shard_map/while/body/eval_jaxpr/reduce_scatter | solution.py:64
  405.6 65.6 %all-gather.33.cloned.1.call-start = ((), (), s32[]{:S(2)}) async-start(), calls=%async_computation.18 | async-start | bytes 1327104 | tf_op jit(solution)/shard_map/while/body/eval_jaxpr/all_gather | solution.py:41
  429.7 83.5 %all-gather.35.cloned.1.call-start = ((), (), s32[]{:S(2)}) async-start(), calls=%async_computation.19 | async-start | bytes 1327104 | tf_op jit(solution)/shard_map/while/body/eval_jaxpr/all_gather | solution.py:39
  430.4 203.3 %reduce-scatter.31.cloned.1.call-start = ((), (), s32[]{:S(2)}) async-start(), calls=%async_computation.20 | async-start | bytes 1105920 | tf_op jit(solution)/shard_map/while/body/eval_jaxpr/reduce_scatter | solution.py:80
  516.6 288.1 %reduce-scatter.33.cloned.1.call-start = ((), (), s32[]{:S(2)}) async-start(), calls=%async_computation.21 | async-start | bytes 1105920 | tf_op jit(solution)/shard_map/while/body/eval_jaxpr/reduce_scatter | solution.py:80
  726.9 26.6 collective-permute-start.8
  736.8 24.0 collective-permute-start.11
  809.7 327.2 %reduce-scatter.27.cloned.1.call-start = ((), (), s32[]{:S(2)}) async-start(), calls=%async_computation.14 | async-start | bytes 1105920 | tf_op jit(solution)/shard_map/while/body/eval_jaxpr/reduce_scatter | solution.py:64
  972.6 74.5 %collective-permute-start.5 = (bf16[576,2,192]{0,2,1:T(8,128)(2,1)S(1)}, bf16[576,2,192]{0,2,1:T(8,128)(2,1)S(1)}, u32[]{:S(2)}, u32[]{:S(2)}) collective-permute-start(bf16[576,2,192]{0,2,1:T(8,128)(2,1)S(1)} %slice.463), channel_id=1, source_target_pairs={{12,0},{16,4},{20,8},{24,12},{28,16},{13,1},{17,5},{21,9},{25,13},... | collective-permute-start | bytes 1327112 | tf_op jit(solution)/shard_map/while/body/eval_jaxpr/ppermute | solution.py:16
  973.9 77.0 %collective-permute-start.4 = (bf16[576,2,192]{0,2,1:T(8,128)(2,1)S(1)}, bf16[576,2,192]{0,2,1:T(8,128)(2,1)S(1)}, u32[]{:S(2)}, u32[]{:S(2)}) collective-permute-start(bf16[576,2,192]{0,2,1:T(8,128)(2,1)S(1)} %slice.463), channel_id=1, source_target_pairs={{8,0},{12,4},{16,8},{20,12},{24,16},{28,20},{9,1},{13,5},{17,9},{2... | collective-permute-start | bytes 1327112 | tf_op jit(solution)/shard_map/while/body/eval_jaxpr/ppermute | solution.py:16
  975.2 75.7 %collective-permute-start.3 = (bf16[576,2,192]{0,2,1:T(8,128)(2,1)S(1)}, bf16[576,2,192]{0,2,1:T(8,128)(2,1)S(1)}, u32[]{:S(2)}, u32[]{:S(2)}) collective-permute-start(bf16[576,2,192]{0,2,1:T(8,128)(2,1)S(1)} %slice.463), channel_id=1, source_target_pairs={{4,0},{8,4},{12,8},{16,12},{20,16},{24,20},{28,24},{5,1},{9,5},{13... | collective-permute-start | bytes 1327112 | tf_op jit(solution)/shard_map/while/body/eval_jaxpr/ppermute | solution.py:16
  976.5 74.4 %collective-permute-start.2 = (bf16[576,2,192]{0,2,1:T(8,128)(2,1)S(1)}, bf16[576,2,192]{0,2,1:T(8,128)(2,1)}, u32[]{:S(2)}, u32[]{:S(2)}) collective-permute-start(bf16[576,2,192]{0,2,1:T(8,128)(2,1)S(1)} %slice.463), channel_id=1, source_target_pairs={{0,4},{4,8},{8,12},{12,16},{16,20},{20,24},{24,28},{1,5},{5,9},{9,... | collective-permute-start | bytes 1327112 | tf_op jit(solution)/shard_map/while/body/eval_jaxpr/ppermute | solution.py:16
  981.8 69.1 %collective-permute-start.1 = (bf16[576,2,192]{0,2,1:T(8,128)(2,1)S(1)}, bf16[576,2,192]{0,2,1:T(8,128)(2,1)}, u32[]{:S(2)}, u32[]{:S(2)}) collective-permute-start(bf16[576,2,192]{0,2,1:T(8,128)(2,1)S(1)} %slice.463), channel_id=1, source_target_pairs={{0,8},{4,12},{8,16},{12,20},{16,24},{20,28},{1,9},{5,13},{9,17},{1... | collective-permute-start | bytes 1327112 | tf_op jit(solution)/shard_map/while/body/eval_jaxpr/ppermute | solution.py:16
  1107.7 49.4 %all-gather.29.cloned.1.call-start = ((), (), s32[]{:S(2)}) async-start(), calls=%async_computation.15 | async-start | bytes 1327104 | tf_op jit(solution)/shard_map/while/body/eval_jaxpr/all_gather | solution.py:39
  1108.4 90.8 %all-gather.31.cloned.1.call-start = ((), (), s32[]{:S(2)}) async-start(), calls=%async_computation.16 | async-start | bytes 1327104 | tf_op jit(solution)/shard_map/while/body/eval_jaxpr/all_gather | solution.py:41
  1109.2 115.8 %reduce-scatter.29.cloned.1.call-start = ((), (), s32[]{:S(2)}) async-start(), calls=%async_computation.17 | async-start | bytes 1105920 | tf_op jit(solution)/shard_map/while/body/eval_jaxpr/reduce_scatter | solution.py:64
  1202.7 65.6 %all-gather.33.cloned.1.call-start = ((), (), s32[]{:S(2)}) async-start(), calls=%async_computation.18 | async-start | bytes 1327104 | tf_op jit(solution)/shard_map/while/body/eval_jaxpr/all_gather | solution.py:41
  1226.7 83.4 %all-gather.35.cloned.1.call-start = ((), (), s32[]{:S(2)}) async-start(), calls=%async_computation.19 | async-start | bytes 1327104 | tf_op jit(solution)/shard_map/while/body/eval_jaxpr/all_gather | solution.py:39
  1227.3 205.7 %reduce-scatter.31.cloned.1.call-start = ((), (), s32[]{:S(2)}) async-start(), calls=%async_computation.20 | async-start | bytes 1105920 | tf_op jit(solution)/shard_map/while/body/eval_jaxpr/reduce_scatter | solution.py:80
  1313.5 290.6 %reduce-scatter.33.cloned.1.call-start = ((), (), s32[]{:S(2)}) async-start(), calls=%async_computation.21 | async-start | bytes 1105920 | tf_op jit(solution)/shard_map/while/body/eval_jaxpr/reduce_scatter | solution.py:80
  1526.3 26.6 collective-permute-start.8
  1609.0 327.2 %reduce-scatter.27.cloned.1.call-start = ((), (), s32[]{:S(2)}) async-start(), calls=%async_computation.14 | async-start | bytes 1105920 | tf_op jit(solution)/shard_map/while/body/eval_jaxpr/reduce_scatter | solution.py:64
  1771.9 74.5 %collective-permute-start.5 = (bf16[576,2,192]{0,2,1:T(8,128)(2,1)S(1)}, bf16[576,2,192]{0,2,1:T(8,128)(2,1)S(1)}, u32[]{:S(2)}, u32[]{:S(2)}) collective-permute-start(bf16[576,2,192]{0,2,1:T(8,128)(2,1)S(1)} %slice.463), channel_id=1, source_target_pairs={{12,0},{16,4},{20,8},{24,12},{28,16},{13,1},{17,5},{21,9},{25,13},... | collective-permute-start | bytes 1327112 | tf_op jit(solution)/shard_map/while/body/eval_jaxpr/ppermute | solution.py:16
  1773.2 77.0 %collective-permute-start.4 = (bf16[576,2,192]{0,2,1:T(8,128)(2,1)S(1)}, bf16[576,2,192]{0,2,1:T(8,128)(2,1)S(1)}, u32[]{:S(2)}, u32[]{:S(2)}) collective-permute-start(bf16[576,2,192]{0,2,1:T(8,128)(2,1)S(1)} %slice.463), channel_id=1, source_target_pairs={{8,0},{12,4},{16,8},{20,12},{24,16},{28,20},{9,1},{13,5},{17,9},{2... | collective-permute-start | bytes 1327112 | tf_op jit(solution)/shard_map/while/body/eval_jaxpr/ppermute | solution.py:16
  1774.5 75.7 %collective-permute-start.3 = (bf16[576,2,192]{0,2,1:T(8,128)(2,1)S(1)}, bf16[576,2,192]{0,2,1:T(8,128)(2,1)S(1)}, u32[]{:S(2)}, u32[]{:S(2)}) collective-permute-start(bf16[576,2,192]{0,2,1:T(8,128)(2,1)S(1)} %slice.463), channel_id=1, source_target_pairs={{4,0},{8,4},{12,8},{16,12},{20,16},{24,20},{28,24},{5,1},{9,5},{13... | collective-permute-start | bytes 1327112 | tf_op jit(solution)/shard_map/while/body/eval_jaxpr/ppermute | solution.py:16
  1775.8 74.4 %collective-permute-start.2 = (bf16[576,2,192]{0,2,1:T(8,128)(2,1)S(1)}, bf16[576,2,192]{0,2,1:T(8,128)(2,1)}, u32[]{:S(2)}, u32[]{:S(2)}) collective-permute-start(bf16[576,2,192]{0,2,1:T(8,128)(2,1)S(1)} %slice.463), channel_id=1, source_target_pairs={{0,4},{4,8},{8,12},{12,16},{16,20},{20,24},{24,28},{1,5},{5,9},{9,... | collective-permute-start | bytes 1327112 | tf_op jit(solution)/shard_map/while/body/eval_jaxpr/ppermute | solution.py:16
  1781.1 69.1 %collective-permute-start.1 = (bf16[576,2,192]{0,2,1:T(8,128)(2,1)S(1)}, bf16[576,2,192]{0,2,1:T(8,128)(2,1)}, u32[]{:S(2)}, u32[]{:S(2)}) collective-permute-start(bf16[576,2,192]{0,2,1:T(8,128)(2,1)S(1)} %slice.463), channel_id=1, source_target_pairs={{0,8},{4,12},{8,16},{12,20},{16,24},{20,28},{1,9},{5,13},{9,17},{1... | collective-permute-start | bytes 1327112 | tf_op jit(solution)/shard_map/while/body/eval_jaxpr/ppermute | solution.py:16
  1907.0 49.3 %all-gather.29.cloned.1.call-start = ((), (), s32[]{:S(2)}) async-start(), calls=%async_computation.15 | async-start | bytes 1327104 | tf_op jit(solution)/shard_map/while/body/eval_jaxpr/all_gather | solution.py:39
  1907.6 90.7 %all-gather.31.cloned.1.call-start = ((), (), s32[]{:S(2)}) async-start(), calls=%async_computation.16 | async-start | bytes 1327104 | tf_op jit(solution)/shard_map/while/body/eval_jaxpr/all_gather | solution.py:41
  1908.4 115.7 %reduce-scatter.29.cloned.1.call-start = ((), (), s32[]{:S(2)}) async-start(), calls=%async_computation.17 | async-start | bytes 1105920 | tf_op jit(solution)/shard_map/while/body/eval_jaxpr/reduce_scatter | solution.py:64
  2001.7 65.6 %all-gather.33.cloned.1.call-start = ((), (), s32[]{:S(2)}) async-start(), calls=%async_computation.18 | async-start | bytes 1327104 | tf_op jit(solution)/shard_map/while/body/eval_jaxpr/all_gather | solution.py:41
  2025.8 83.5 %all-gather.35.cloned.1.call-start = ((), (), s32[]{:S(2)}) async-start(), calls=%async_computation.19 | async-start | bytes 1327104 | tf_op jit(solution)/shard_map/while/body/eval_jaxpr/all_gather | solution.py:39
  2026.6 205.7 %reduce-scatter.31.cloned.1.call-start = ((), (), s32[]{:S(2)}) async-start(), calls=%async_computation.20 | async-start | bytes 1105920 | tf_op jit(solution)/shard_map/while/body/eval_jaxpr/reduce_scatter | solution.py:80
  2112.7 290.6 %reduce-scatter.33.cloned.1.call-start = ((), (), s32[]{:S(2)}) async-start(), calls=%async_computation.21 | async-start | bytes 1105920 | tf_op jit(solution)/shard_map/while/body/eval_jaxpr/reduce_scatter | solution.py:80
  2325.6 26.6 collective-permute-start.8
  2335.5 24.0 collective-permute-start.11
  2408.3 327.2 %reduce-scatter.27.cloned.1.call-start = ((), (), s32[]{:S(2)}) async-start(), calls=%async_computation.14 | async-start | bytes 1105920 | tf_op jit(solution)/shard_map/while/body/eval_jaxpr/reduce_scatter | solution.py:64
  2571.2 74.5 %collective-permute-start.5 = (bf16[576,2,192]{0,2,1:T(8,128)(2,1)S(1)}, bf16[576,2,192]{0,2,1:T(8,128)(2,1)S(1)}, u32[]{:S(2)}, u32[]{:S(2)}) collective-permute-start(bf16[576,2,192]{0,2,1:T(8,128)(2,1)S(1)} %slice.463), channel_id=1, source_target_pairs={{12,0},{16,4},{20,8},{24,12},{28,16},{13,1},{17,5},{21,9},{25,13},... | collective-permute-start | bytes 1327112 | tf_op jit(solution)/shard_map/while/body/eval_jaxpr/ppermute | solution.py:16
  2572.5 77.0 %collective-permute-start.4 = (bf16[576,2,192]{0,2,1:T(8,128)(2,1)S(1)}, bf16[576,2,192]{0,2,1:T(8,128)(2,1)S(1)}, u32[]{:S(2)}, u32[]{:S(2)}) collective-permute-start(bf16[576,2,192]{0,2,1:T(8,128)(2,1)S(1)} %slice.463), channel_id=1, source_target_pairs={{8,0},{12,4},{16,8},{20,12},{24,16},{28,20},{9,1},{13,5},{17,9},{2... | collective-permute-start | bytes 1327112 | tf_op jit(solution)/shard_map/while/body/eval_jaxpr/ppermute | solution.py:16
  2573.8 75.7 %collective-permute-start.3 = (bf16[576,2,192]{0,2,1:T(8,128)(2,1)S(1)}, bf16[576,2,192]{0,2,1:T(8,128)(2,1)S(1)}, u32[]{:S(2)}, u32[]{:S(2)}) collective-permute-start(bf16[576,2,192]{0,2,1:T(8,128)(2,1)S(1)} %slice.463), channel_id=1, source_target_pairs={{4,0},{8,4},{12,8},{16,12},{20,16},{24,20},{28,24},{5,1},{9,5},{13... | collective-permute-start | bytes 1327112 | tf_op jit(solution)/shard_map/while/body/eval_jaxpr/ppermute | solution.py:16
  2575.1 74.4 %collective-permute-start.2 = (bf16[576,2,192]{0,2,1:T(8,128)(2,1)S(1)}, bf16[576,2,192]{0,2,1:T(8,128)(2,1)}, u32[]{:S(2)}, u32[]{:S(2)}) collective-permute-start(bf16[576,2,192]{0,2,1:T(8,128)(2,1)S(1)} %slice.463), channel_id=1, source_target_pairs={{0,4},{4,8},{8,12},{12,16},{16,20},{20,24},{24,28},{1,5},{5,9},{9,... | collective-permute-start | bytes 1327112 | tf_op jit(solution)/shard_map/while/body/eval_jaxpr/ppermute | solution.py:16
  2580.4 69.1 %collective-permute-start.1 = (bf16[576,2,192]{0,2,1:T(8,128)(2,1)S(1)}, bf16[576,2,192]{0,2,1:T(8,128)(2,1)}, u32[]{:S(2)}, u32[]{:S(2)}) collective-permute-start(bf16[576,2,192]{0,2,1:T(8,128)(2,1)S(1)} %slice.463), channel_id=1, source_target_pairs={{0,8},{4,12},{8,16},{12,20},{16,24},{20,28},{1,9},{5,13},{9,17},{1... | collective-permute-start | bytes 1327112 | tf_op jit(solution)/shard_map/while/body/eval_jaxpr/ppermute | solution.py:16
  2706.3 49.2 %all-gather.29.cloned.1.call-start = ((), (), s32[]{:S(2)}) async-start(), calls=%async_computation.15 | async-start | bytes 1327104 | tf_op jit(solution)/shard_map/while/body/eval_jaxpr/all_gather | solution.py:39
  2706.9 90.6 %all-gather.31.cloned.1.call-start = ((), (), s32[]{:S(2)}) async-start(), calls=%async_computation.16 | async-start | bytes 1327104 | tf_op jit(solution)/shard_map/while/body/eval_jaxpr/all_gather | solution.py:41
  2707.6 115.6 %reduce-scatter.29.cloned.1.call-start = ((), (), s32[]{:S(2)}) async-start(), calls=%async_computation.17 | async-start | bytes 1105920 | tf_op jit(solution)/shard_map/while/body/eval_jaxpr/reduce_scatter | solution.py:64
  2800.9 65.6 %all-gather.33.cloned.1.call-start = ((), (), s32[]{:S(2)}) async-start(), calls=%async_computation.18 | async-start | bytes 1327104 | tf_op jit(solution)/shard_map/while/body/eval_jaxpr/all_gather | solution.py:41
  2825.0 83.5 %all-gather.35.cloned.1.call-start = ((), (), s32[]{:S(2)}) async-start(), calls=%async_computation.19 | async-start | bytes 1327104 | tf_op jit(solution)/shard_map/while/body/eval_jaxpr/all_gather | solution.py:39
  2825.8 205.7 %reduce-scatter.31.cloned.1.call-start = ((), (), s32[]{:S(2)}) async-start(), calls=%async_computation.20 | async-start | bytes 1105920 | tf_op jit(solution)/shard_map/while/body/eval_jaxpr/reduce_scatter | solution.py:80
  2911.9 290.6 %reduce-scatter.33.cloned.1.call-start = ((), (), s32[]{:S(2)}) async-start(), calls=%async_computation.21 | async-start | bytes 1105920 | tf_op jit(solution)/shard_map/while/body/eval_jaxpr/reduce_scatter | solution.py:80
  3124.7 26.7 collective-permute-start.8
  3134.6 24.0 collective-permute-start.11
  3209.7 73.2 %reduce-scatter.25.cloned.1.call-start = ((), (), s32[]{:S(2)}) async-start(), calls=%async_computation.13 | async-start | bytes 442368
  3211.4 129.8 %reduce-scatter.23.cloned.1.call-start = ((), (), s32[]{:S(2)}) async-start(), calls=%async_computation.12 | async-start | bytes 884736
  3213.7 200.3 %reduce-scatter.17.cloned.1.call-start = ((), (), s32[]{:S(2)}) async-start(), calls=%async_computation.9 | async-start | bytes 2654208 | tf_op jit(solution)/shard_map/reduce_scatter | solution.py:341
  3216.8 270.0 %reduce-scatter.19.cloned.1.call-start = ((), (), s32[]{:S(2)}) async-start(), calls=%async_computation.10 | async-start | bytes 2654208 | tf_op jit(solution)/shard_map/reduce_scatter | solution.py:344
  3217.4 342.6 %reduce-scatter.21.cloned.1.call-start = ((), (), s32[]{:S(2)}) async-start(), calls=%async_computation.11 | async-start | bytes 2654208 | tf_op jit(solution)/shard_map/reduce_scatter | solution.py:346
  (334 other events, 7935.7 us)
Sparse Core Ops, SparseCore 0:
  311.3 29.0 reduce-scatter.26
  405.7 22.1 reduce-scatter.28
  516.7 22.1 reduce-scatter.30
  763.5 41.1 reduce-scatter.32
  1107.8 29.0 reduce-scatter.26
  1202.8 22.1 reduce-scatter.28
  1313.6 22.1 reduce-scatter.30
  1562.9 41.1 reduce-scatter.32
  1907.2 29.0 reduce-scatter.26
  2001.9 22.1 reduce-scatter.28
  2112.9 22.1 reduce-scatter.30
  2362.1 41.1 reduce-scatter.32
  2706.4 29.0 reduce-scatter.26
  2801.1 22.1 reduce-scatter.28
  2912.1 22.1 reduce-scatter.30
  3161.3 41.1 reduce-scatter.32
  3213.5 62.2 reduce-scatter.24
  3278.9 62.2 reduce-scatter.22
  3345.3 68.7 reduce-scatter.16
  3418.0 68.8 reduce-scatter.18
  3490.9 68.9 reduce-scatter.20
Sparse Core Ops, SparseCore 1:
  313.9 46.4 all-gather.28
  362.4 39.7 all-gather.30
  429.8 41.4 all-gather.32
  473.4 39.7 all-gather.34
  1110.7 46.4 all-gather.28
  1159.3 39.9 all-gather.30
  1226.8 41.4 all-gather.32
  1270.3 39.7 all-gather.34
  1909.7 46.5 all-gather.28
  1958.5 39.7 all-gather.30
  2025.9 41.4 all-gather.32
  2069.6 39.7 all-gather.34
  2709.0 46.5 all-gather.28
  2757.7 39.7 all-gather.30
  2825.1 41.4 all-gather.32
  2868.8 39.7 all-gather.34
where the time goes:
time: 3580 us; the launch traced here: 3570 us
  blocking collectives  1450 us (41%)
  waiting for transfers between devices  1050 us (29%)
  matrix products  374 us (10%)
  other arithmetic  347 us (10%)
  local copies, waits for them, and re-layouts  193 us (5%)
  starting transfers between devices  122 us (3%)
    all_gather x8, blocking collectives, fetch_weights(): lax.all_gather(gains, ('dp', 'mp'), axis=1, tiled=True)  321 us
    all_gather x8, blocking collectives, fetch_weights(): lax.all_gather(w_qkv, 'dp', axis=0, tiled=True)  296 us
    all_gather x8, blocking collectives, fetch_weights(): lax.all_gather(w_out, 'dp', axis=1, tiled=True)  267 us
    all_gather x8, waiting for transfers between devices, fetch_weights(): lax.all_gather(w_down, 'dp', axis=1, tiled=True)  260 us
    all_gather x8, waiting for transfers between devices, fetch_weights(): lax.all_gather(w_up, 'dp', axis=0, tiled=True)  175 us
    all_gather x4, blocking collectives, fetch_weights(): lax.all_gather(biases, ('dp', 'mp'), axis=1, tiled=True)  148 us
    convert_element_type x12, other arithmetic, backward_pass(): grad_scores = (soft_weights * (grad_soft - row_delta)).astype(jnp.bfloat16)  139 us
    reduce_scatter x8, waiting for transfers between devices, project_back(): lax.psum_scatter(term(jnp.int32(0), share_rows * lax.axis_size('mp')).ast...  135 us
  transfers between devices with their start and end apart: 85, of which 52 were waited for; matrix products, arithmetic and copies ran while one was open for 8% of the time, Pallas kernels for 0%

commit v1 on v0

--- a/solution.py
+++ b/solution.py
@@ -1,3 +1,4 @@
+import functools
 import jax
 import jax.numpy as jnp
 from jax import lax
@@ -8,6 +9,24 @@
 CLIP = 1500
 epsilon = 1e-05
 masked_score = -1e30
+
+
+def unite_region(local_values, lane_axis, k_dim):
+    wide_out = lax.axis_size(lane_axis)
+    block_now = lax.axis_index(lane_axis)
+    small, m_next, even = (wide_out, block_now, local_values.shape[k_dim])
+    x_next, outer = (local_values, 1)
+    while outer < small:
+        spare = range(small)
+        current_block = map(lambda j: (j, (j - outer) % small), spare)
+        z_new = list(current_block)
+        formed = lax.ppermute(x_next, lane_axis, z_new)
+        x_next = jnp.concatenate([x_next, formed], k_dim)
+        outer = 2 * outer
+    return jnp.roll(x_next, m_next * even, k_dim)
+
+
+serve_numbers = functools.partial(unite_region, lane_axis=("dp", "mp"), k_dim=1)
 
 
 def passed_along(array, axis, by):
@@ -40,10 +59,7 @@
         lax.all_gather(b_up, "dp", axis=1, tiled=True),
         lax.all_gather(w_down, "dp", axis=1, tiled=True),
     )
-    norm_rows = (
-        lax.all_gather(gains, ("dp", "mp"), axis=1, tiled=True),
-        lax.all_gather(biases, ("dp", "mp"), axis=1, tiled=True),
-    )
+    norm_rows = (lax.all_gather(gains, ("dp", "mp"), axis=1, tiled=True), serve_numbers(biases))
     return (gathered, norm_rows)
 
 

time: 3580 us -> 3470 us (0.969)
  blocking collectives: 1450 us -> 1300 us
    all_gather x4 -> x0, blocking collectives: 148 us -> none  [fetch_weights(): lax.all_gather(biases, ('dp', 'mp'), axis=1, tiled=True)]
  transfers between devices with their start and end apart: 85 -> 90, of which waited for: 52 -> 57; matrix products, arithmetic and copies ran while one was open for 8% -> 8% of each run, Pallas kernels for 0% -> 0%
where the time goes in v1:
time: 3470 us; the launch traced here: 3460 us
  blocking collectives  1300 us (37%)
  waiting for transfers between devices  1070 us (31%)
  matrix products  375 us (11%)
  other arithmetic  352 us (10%)
  local copies, waits for them, and re-layouts  201 us (6%)
  starting transfers between devices  130 us (4%)
    all_gather x8, blocking collectives, fetch_weights(): lax.all_gather(gains, ('dp', 'mp'), axis=1, tiled=True)  323 us
    all_gather x8, blocking collectives, fetch_weights(): lax.all_gather(w_qkv, 'dp', axis=0, tiled=True)  298 us
    all_gather x8, blocking collectives, fetch_weights(): lax.all_gather(w_out, 'dp', axis=1, tiled=True)  268 us
    all_gather x8, waiting for transfers between devices, fetch_weights(): lax.all_gather(w_down, 'dp', axis=1, tiled=True)  260 us
    all_gather x8, waiting for transfers between devices, fetch_weights(): lax.all_gather(w_up, 'dp', axis=0, tiled=True)  175 us
    convert_element_type x12, other arithmetic, backward_pass(): grad_scores = (soft_weights * (grad_soft - row_delta)).astype(jnp.bfloat16)  138 us
    reduce_scatter x8, waiting for transfers between devices, project_back(): lax.psum_scatter(term(jnp.int32(0), share_rows * lax.axis_size('mp')).ast...  135 us
    all_gather x4, blocking collectives, fetch_weights(): lax.all_gather(b_qv, 'dp', axis=2, tiled=True)  122 us
  transfers between devices with their start and end apart: 90, of which 57 were waited for; matrix products, arithmetic and copies ran while one was open for 8% of the time, Pallas kernels for 0%

profile of v1, /device:TPU:0, one launch (start us, length us, event | category | flops | bytes accessed | tf_op | source)
XLA Modules:
  0.0 3457.9 jit_solution(3565876906079245996)
XLA Ops:
  35.8 3063.9 %while.33 = (s32[]{:T(128)}, f32[768,3,192]{0,2,1:T(8,128)}, f32[2,1,192]{2,1,0:T(1,128)}, f32[192,768]{1,0:T(8,128)}, f32[768,768]{1,0:T(8,128)}, /*index=5*/f3...) while((s32[]{:T(128)}, f32[768,3,192]{0,2,1:T(8,128)}, ...), condition=%wide.region_31.32_spmd.clone.clone.clone, body=%wide.region_0.31_spmd.clone.clone.clone.sunk | while | flops 11638809600 | bytes 781708416 | solution.py:355
  40.0 45.1 %all-gather.15 = bf16[32,24,2]{1,2,0:T(2,128)(2,1)S(1)} all-gather(bf16[1,24,2]{1,2,0:T(2,128)(2,1)} %bitcast.326), channel_id=1, replica_groups=mesh['dp'=8,'mp'=4] {'dp','mp'}, dimensions={0}, use_global_device_ids=true | all-gather | bytes 3168 | tf_op jit(solution)/shard_map/while/body/eval_jaxpr/all_gather | solution.py:62
  86.0 30.5 all_gather.146
  127.4 37.6 %all_gather.144 = bf16[768,3,192]{2,1,0:T(4,128)(2,1)S(1)} all-gather(bf16[96,3,192]{2,1,0:T(4,128)(2,1)S(1)} %copy.78), channel_id=1, replica_groups=mesh['dp'=8,'mp'=4] {'dp'}, dimensions={0}, use_global_device_ids=true | all-gather | bytes 995328 | tf_op jit(solution)/shard_map/while/body/eval_jaxpr/all_gather | solution.py:55
  185.5 22.7 gather_fusion
  208.3 33.3 all_gather.147
  305.3 23.7 all-reduce.9
  361.0 34.0 all-gather.25.cloned.1.call-done
  398.4 22.3 reduce-scatter.29.cloned.1.call-done
  433.3 30.7 all-gather.27.cloned.1.call-done
  469.5 36.6 %all-gather.29.cloned.1.call-done = bf16[768,768]{1,0:T(8,128)(2,1)} async-done(((bf16[96,768]{1,0:T(8,128)(2,1)}), bf16[768,768]{1,0:T(8,128)(2,1)}) %all-gather.29.cloned.1.call-update) | async-done | bytes 1179664 | tf_op jit(solution)/shard_map/while/body/eval_jaxpr/all_gather | solution.py:58
  514.0 38.9 %all-gather.17 = bf16[32,24,2]{1,2,0:T(2,128)(2,1)S(1)} all-gather(bf16[1,24,2]{1,2,0:T(2,128)(2,1)S(1)} %bitcast.327), channel_id=1, replica_groups=mesh['dp'=8,'mp'=4] {'dp','mp'}, dimensions={0}, use_global_device_ids=true | all-gather | bytes 3168 | tf_op jit(solution)/shard_map/while/body/eval_jaxpr/all_gather | solution.py:62
  553.2 33.6 all_gather.154
  586.9 37.0 %all_gather.155 = bf16[768,3,192]{2,0,1:T(8,128)(2,1)} all-gather(bf16[96,3,192]{2,0,1:T(8,128)(2,1)S(1)} %copy-done.32), channel_id=1, replica_groups=mesh['dp'=8,'mp'=4] {'dp'}, dimensions={0}, use_global_device_ids=true | all-gather | bytes 995328 | tf_op jit(solution)/shard_map/while/body/eval_jaxpr/all_gather | solution.py:55
  762.8 35.0 %reduce-scatter.33.cloned.1.call-done = bf16[144,768]{1,0:T(8,128)(2,1)} async-done(((bf16[576,768]{1,0:T(8,128)(2,1)}), bf16[144,768]{1,0:T(8,128)(2,1)}) %reduce-scatter.33.cloned.1.call-update) | async-done | bytes 221200 | tf_op jit(solution)/shard_map/while/body/eval_jaxpr/reduce_scatter | solution.py:96
  806.9 40.7 %all-gather.15 = bf16[32,24,2]{1,2,0:T(2,128)(2,1)S(1)} all-gather(bf16[1,24,2]{1,2,0:T(2,128)(2,1)} %bitcast.326), channel_id=1, replica_groups=mesh['dp'=8,'mp'=4] {'dp','mp'}, dimensions={0}, use_global_device_ids=true | all-gather | bytes 3168 | tf_op jit(solution)/shard_map/while/body/eval_jaxpr/all_gather | solution.py:62
  848.5 30.5 all_gather.146
  890.0 37.6 %all_gather.144 = bf16[768,3,192]{2,1,0:T(4,128)(2,1)S(1)} all-gather(bf16[96,3,192]{2,1,0:T(4,128)(2,1)S(1)} %copy.78), channel_id=1, replica_groups=mesh['dp'=8,'mp'=4] {'dp'}, dimensions={0}, use_global_device_ids=true | all-gather | bytes 995328 | tf_op jit(solution)/shard_map/while/body/eval_jaxpr/all_gather | solution.py:55
  948.1 22.7 gather_fusion
  970.8 33.3 all_gather.147
  1067.9 23.6 all-reduce.9
  1123.4 34.3 all-gather.25.cloned.1.call-done
  1161.2 22.3 reduce-scatter.29.cloned.1.call-done
  1195.9 30.9 all-gather.27.cloned.1.call-done
  1232.2 36.4 %all-gather.29.cloned.1.call-done = bf16[768,768]{1,0:T(8,128)(2,1)} async-done(((bf16[96,768]{1,0:T(8,128)(2,1)}), bf16[768,768]{1,0:T(8,128)(2,1)}) %all-gather.29.cloned.1.call-update) | async-done | bytes 1179664 | tf_op jit(solution)/shard_map/while/body/eval_jaxpr/all_gather | solution.py:58
  1277.4 38.9 %all-gather.17 = bf16[32,24,2]{1,2,0:T(2,128)(2,1)S(1)} all-gather(bf16[1,24,2]{1,2,0:T(2,128)(2,1)S(1)} %bitcast.327), channel_id=1, replica_groups=mesh['dp'=8,'mp'=4] {'dp','mp'}, dimensions={0}, use_global_device_ids=true | all-gather | bytes 3168 | tf_op jit(solution)/shard_map/while/body/eval_jaxpr/all_gather | solution.py:62
  1316.6 33.6 all_gather.154
  1350.2 37.0 %all_gather.155 = bf16[768,3,192]{2,0,1:T(8,128)(2,1)} all-gather(bf16[96,3,192]{2,0,1:T(8,128)(2,1)S(1)} %copy-done.32), channel_id=1, replica_groups=mesh['dp'=8,'mp'=4] {'dp'}, dimensions={0}, use_global_device_ids=true | all-gather | bytes 995328 | tf_op jit(solution)/shard_map/while/body/eval_jaxpr/all_gather | solution.py:55
  1448.4 11.6 multiply_convert_fusion.10
  1529.6 33.2 reduce-scatter.33.cloned.1.call-done
  1572.0 40.7 %all-gather.15 = bf16[32,24,2]{1,2,0:T(2,128)(2,1)S(1)} all-gather(bf16[1,24,2]{1,2,0:T(2,128)(2,1)} %bitcast.326), channel_id=1, replica_groups=mesh['dp'=8,'mp'=4] {'dp','mp'}, dimensions={0}, use_global_device_ids=true | all-gather | bytes 3168 | tf_op jit(solution)/shard_map/while/body/eval_jaxpr/all_gather | solution.py:62
  1613.6 30.5 all_gather.146
  1655.0 37.6 %all_gather.144 = bf16[768,3,192]{2,1,0:T(4,128)(2,1)S(1)} all-gather(bf16[96,3,192]{2,1,0:T(4,128)(2,1)S(1)} %copy.78), channel_id=1, replica_groups=mesh['dp'=8,'mp'=4] {'dp'}, dimensions={0}, use_global_device_ids=true | all-gather | bytes 995328 | tf_op jit(solution)/shard_map/while/body/eval_jaxpr/all_gather | solution.py:55
  1713.1 22.7 gather_fusion
  1735.9 33.3 all_gather.147
  1832.8 23.5 all-reduce.9
  1888.3 34.1 all-gather.25.cloned.1.call-done
  1925.8 22.3 reduce-scatter.29.cloned.1.call-done
  1960.7 30.7 all-gather.27.cloned.1.call-done
  1996.8 36.6 %all-gather.29.cloned.1.call-done = bf16[768,768]{1,0:T(8,128)(2,1)} async-done(((bf16[96,768]{1,0:T(8,128)(2,1)}), bf16[768,768]{1,0:T(8,128)(2,1)}) %all-gather.29.cloned.1.call-update) | async-done | bytes 1179664 | tf_op jit(solution)/shard_map/while/body/eval_jaxpr/all_gather | solution.py:58
  2042.2 38.9 %all-gather.17 = bf16[32,24,2]{1,2,0:T(2,128)(2,1)S(1)} all-gather(bf16[1,24,2]{1,2,0:T(2,128)(2,1)S(1)} %bitcast.327), channel_id=1, replica_groups=mesh['dp'=8,'mp'=4] {'dp','mp'}, dimensions={0}, use_global_device_ids=true | all-gather | bytes 3168 | tf_op jit(solution)/shard_map/while/body/eval_jaxpr/all_gather | solution.py:62
  2081.4 33.6 all_gather.154
  2115.0 37.0 %all_gather.155 = bf16[768,3,192]{2,0,1:T(8,128)(2,1)} all-gather(bf16[96,3,192]{2,0,1:T(8,128)(2,1)S(1)} %copy-done.32), channel_id=1, replica_groups=mesh['dp'=8,'mp'=4] {'dp'}, dimensions={0}, use_global_device_ids=true | all-gather | bytes 995328 | tf_op jit(solution)/shard_map/while/body/eval_jaxpr/all_gather | solution.py:55
  2294.4 33.2 reduce-scatter.33.cloned.1.call-done
  2336.8 40.7 %all-gather.15 = bf16[32,24,2]{1,2,0:T(2,128)(2,1)S(1)} all-gather(bf16[1,24,2]{1,2,0:T(2,128)(2,1)} %bitcast.326), channel_id=1, replica_groups=mesh['dp'=8,'mp'=4] {'dp','mp'}, dimensions={0}, use_global_device_ids=true | all-gather | bytes 3168 | tf_op jit(solution)/shard_map/while/body/eval_jaxpr/all_gather | solution.py:62
  2378.4 30.5 all_gather.146
  2419.8 37.6 %all_gather.144 = bf16[768,3,192]{2,1,0:T(4,128)(2,1)S(1)} all-gather(bf16[96,3,192]{2,1,0:T(4,128)(2,1)S(1)} %copy.78), channel_id=1, replica_groups=mesh['dp'=8,'mp'=4] {'dp'}, dimensions={0}, use_global_device_ids=true | all-gather | bytes 995328 | tf_op jit(solution)/shard_map/while/body/eval_jaxpr/all_gather | solution.py:55
  2478.0 22.7 gather_fusion
  2500.7 33.3 all_gather.147
  2597.6 23.5 all-reduce.9
  2653.1 34.1 all-gather.25.cloned.1.call-done
  2690.7 22.3 reduce-scatter.29.cloned.1.call-done
  2725.5 30.7 all-gather.27.cloned.1.call-done
  2761.7 36.6 %all-gather.29.cloned.1.call-done = bf16[768,768]{1,0:T(8,128)(2,1)} async-done(((bf16[96,768]{1,0:T(8,128)(2,1)}), bf16[768,768]{1,0:T(8,128)(2,1)}) %all-gather.29.cloned.1.call-update) | async-done | bytes 1179664 | tf_op jit(solution)/shard_map/while/body/eval_jaxpr/all_gather | solution.py:58
  2807.1 38.9 %all-gather.17 = bf16[32,24,2]{1,2,0:T(2,128)(2,1)S(1)} all-gather(bf16[1,24,2]{1,2,0:T(2,128)(2,1)S(1)} %bitcast.327), channel_id=1, replica_groups=mesh['dp'=8,'mp'=4] {'dp','mp'}, dimensions={0}, use_global_device_ids=true | all-gather | bytes 3168 | tf_op jit(solution)/shard_map/while/body/eval_jaxpr/all_gather | solution.py:62
  2846.3 33.6 all_gather.154
  2879.9 37.0 %all_gather.155 = bf16[768,3,192]{2,0,1:T(8,128)(2,1)} all-gather(bf16[96,3,192]{2,0,1:T(8,128)(2,1)S(1)} %copy-done.32), channel_id=1, replica_groups=mesh['dp'=8,'mp'=4] {'dp'}, dimensions={0}, use_global_device_ids=true | all-gather | bytes 995328 | tf_op jit(solution)/shard_map/while/body/eval_jaxpr/all_gather | solution.py:55
  3059.2 33.2 reduce-scatter.33.cloned.1.call-done
  3112.3 21.4 all-reduce.4
  3133.7 37.3 %all-reduce.7 = (f32[2,768]{1,0:T(2,128)S(1)}, f32[4,768]{1,0:T(4,128)S(1)}) all-reduce(f32[2,768]{1,0:T(2,128)S(1)} %copy-done.57, f32[4,768]{1,0:T(4,128)S(1)} %copy-done.42), channel_id=13, replica_groups=mesh['dp'=8,'mp'=4] {'dp','mp'}, use_global_device_ids=true, to_apply=%region_38.39.clone | all-reduce | flops 4608 | bytes 36864
  3174.4 56.8 %reduce-scatter.23.cloned.1.call-done = f32[96,192]{1,0:T(8,128)} async-done(((f32[768,192]{1,0:T(8,128)}), f32[96,192]{1,0:T(8,128)}) %reduce-scatter.23.cloned.1.call-update) | async-done | bytes 73744
  3232.8 71.0 %reduce-scatter.17.cloned.1.call-done = f32[96,3,192]{2,0,1:T(8,128)} async-done(((f32[768,3,192]{2,0,1:T(8,128)}), f32[96,3,192]{2,0,1:T(8,128)}) %reduce-scatter.17.cloned.1.call-update) | async-done | bytes 221200 | tf_op jit(solution)/shard_map/reduce_scatter | solution.py:357
  3303.9 73.0 %reduce-scatter.19.cloned.1.call-done = f32[96,768]{1,0:T(8,128)} async-done(((f32[768,768]{1,0:T(8,128)}), f32[96,768]{1,0:T(8,128)}) %reduce-scatter.19.cloned.1.call-update) | async-done | bytes 294928 | tf_op jit(solution)/shard_map/reduce_scatter | solution.py:360
  3376.8 73.0 %reduce-scatter.21.cloned.1.call-done = f32[768,96]{0,1:T(8,128)} async-done(((f32[768,768]{0,1:T(8,128)}), f32[768,96]{0,1:T(8,128)}) %reduce-scatter.21.cloned.1.call-update) | async-done | bytes 294928 | tf_op jit(solution)/shard_map/reduce_scatter | solution.py:362
  (1381 shorter events, 1258.8 us)
Async XLA Ops:
  35.8 297.4 %reduce-scatter.27.cloned.1.call-start = ((), (), s32[]{:S(2)}) async-start(), calls=%async_computation.14 | async-start | bytes 1105920 | tf_op jit(solution)/shard_map/while/body/eval_jaxpr/reduce_scatter | solution.py:80
  167.0 74.6 %collective-permute-start.5 = (bf16[576,2,192]{0,2,1:T(8,128)(2,1)S(1)}, bf16[576,2,192]{0,2,1:T(8,128)(2,1)S(1)}, u32[]{:S(2)}, u32[]{:S(2)}) collective-permute-start(bf16[576,2,192]{0,2,1:T(8,128)(2,1)S(1)} %slice.568), channel_id=1, source_target_pairs={{12,0},{16,4},{20,8},{24,12},{28,16},{13,1},{17,5},{21,9},{25,13},... | collective-permute-start | bytes 1327112 | tf_op jit(solution)/shard_map/while/body/eval_jaxpr/ppermute | solution.py:35
  168.3 77.0 %collective-permute-start.4 = (bf16[576,2,192]{0,2,1:T(8,128)(2,1)S(1)}, bf16[576,2,192]{0,2,1:T(8,128)(2,1)S(1)}, u32[]{:S(2)}, u32[]{:S(2)}) collective-permute-start(bf16[576,2,192]{0,2,1:T(8,128)(2,1)S(1)} %slice.568), channel_id=1, source_target_pairs={{8,0},{12,4},{16,8},{20,12},{24,16},{28,20},{9,1},{13,5},{17,9},{2... | collective-permute-start | bytes 1327112 | tf_op jit(solution)/shard_map/while/body/eval_jaxpr/ppermute | solution.py:35
  169.6 75.8 %collective-permute-start.3 = (bf16[576,2,192]{0,2,1:T(8,128)(2,1)S(1)}, bf16[576,2,192]{0,2,1:T(8,128)(2,1)S(1)}, u32[]{:S(2)}, u32[]{:S(2)}) collective-permute-start(bf16[576,2,192]{0,2,1:T(8,128)(2,1)S(1)} %slice.568), channel_id=1, source_target_pairs={{4,0},{8,4},{12,8},{16,12},{20,16},{24,20},{28,24},{5,1},{9,5},{13... | collective-permute-start | bytes 1327112 | tf_op jit(solution)/shard_map/while/body/eval_jaxpr/ppermute | solution.py:35
  170.9 74.5 %collective-permute-start.2 = (bf16[576,2,192]{0,2,1:T(8,128)(2,1)S(1)}, bf16[576,2,192]{0,2,1:T(8,128)(2,1)}, u32[]{:S(2)}, u32[]{:S(2)}) collective-permute-start(bf16[576,2,192]{0,2,1:T(8,128)(2,1)S(1)} %slice.568), channel_id=1, source_target_pairs={{0,4},{4,8},{8,12},{12,16},{16,20},{20,24},{24,28},{1,5},{5,9},{9,... | collective-permute-start | bytes 1327112 | tf_op jit(solution)/shard_map/while/body/eval_jaxpr/ppermute | solution.py:35
  176.3 69.1 %collective-permute-start.1 = (bf16[576,2,192]{0,2,1:T(8,128)(2,1)S(1)}, bf16[576,2,192]{0,2,1:T(8,128)(2,1)}, u32[]{:S(2)}, u32[]{:S(2)}) collective-permute-start(bf16[576,2,192]{0,2,1:T(8,128)(2,1)S(1)} %slice.568), channel_id=1, source_target_pairs={{0,8},{4,12},{8,16},{12,20},{16,24},{20,28},{1,9},{5,13},{9,17},{1... | collective-permute-start | bytes 1327112 | tf_op jit(solution)/shard_map/while/body/eval_jaxpr/ppermute | solution.py:35
  302.6 50.5 %all-gather.23.cloned.1.call-start = ((), (), s32[]{:S(2)}) async-start(), calls=%async_computation.15 | async-start | bytes 1327104 | tf_op jit(solution)/shard_map/while/body/eval_jaxpr/all_gather | solution.py:58
  303.2 91.8 %all-gather.25.cloned.1.call-start = ((), (), s32[]{:S(2)}) async-start(), calls=%async_computation.16 | async-start | bytes 1327104 | tf_op jit(solution)/shard_map/while/body/eval_jaxpr/all_gather | solution.py:60
  303.8 117.0 %reduce-scatter.29.cloned.1.call-start = ((), (), s32[]{:S(2)}) async-start(), calls=%async_computation.17 | async-start | bytes 1105920 | tf_op jit(solution)/shard_map/while/body/eval_jaxpr/reduce_scatter | solution.py:80
  398.4 65.6 %all-gather.27.cloned.1.call-start = ((), (), s32[]{:S(2)}) async-start(), calls=%async_computation.18 | async-start | bytes 1327104 | tf_op jit(solution)/shard_map/while/body/eval_jaxpr/all_gather | solution.py:60
  422.5 83.5 %all-gather.29.cloned.1.call-start = ((), (), s32[]{:S(2)}) async-start(), calls=%async_computation.19 | async-start | bytes 1327104 | tf_op jit(solution)/shard_map/while/body/eval_jaxpr/all_gather | solution.py:58
  423.2 203.2 %reduce-scatter.31.cloned.1.call-start = ((), (), s32[]{:S(2)}) async-start(), calls=%async_computation.20 | async-start | bytes 1105920 | tf_op jit(solution)/shard_map/while/body/eval_jaxpr/reduce_scatter | solution.py:96
  509.4 288.4 %reduce-scatter.33.cloned.1.call-start = ((), (), s32[]{:S(2)}) async-start(), calls=%async_computation.21 | async-start | bytes 1105920 | tf_op jit(solution)/shard_map/while/body/eval_jaxpr/reduce_scatter | solution.py:96
  719.9 26.7 collective-permute-start.8
  729.8 24.0 collective-permute-start.11
  802.7 292.6 %reduce-scatter.27.cloned.1.call-start = ((), (), s32[]{:S(2)}) async-start(), calls=%async_computation.14 | async-start | bytes 1105920 | tf_op jit(solution)/shard_map/while/body/eval_jaxpr/reduce_scatter | solution.py:80
  929.5 74.6 %collective-permute-start.5 = (bf16[576,2,192]{0,2,1:T(8,128)(2,1)S(1)}, bf16[576,2,192]{0,2,1:T(8,128)(2,1)S(1)}, u32[]{:S(2)}, u32[]{:S(2)}) collective-permute-start(bf16[576,2,192]{0,2,1:T(8,128)(2,1)S(1)} %slice.568), channel_id=1, source_target_pairs={{12,0},{16,4},{20,8},{24,12},{28,16},{13,1},{17,5},{21,9},{25,13},... | collective-permute-start | bytes 1327112 | tf_op jit(solution)/shard_map/while/body/eval_jaxpr/ppermute | solution.py:35
  930.8 77.1 %collective-permute-start.4 = (bf16[576,2,192]{0,2,1:T(8,128)(2,1)S(1)}, bf16[576,2,192]{0,2,1:T(8,128)(2,1)S(1)}, u32[]{:S(2)}, u32[]{:S(2)}) collective-permute-start(bf16[576,2,192]{0,2,1:T(8,128)(2,1)S(1)} %slice.568), channel_id=1, source_target_pairs={{8,0},{12,4},{16,8},{20,12},{24,16},{28,20},{9,1},{13,5},{17,9},{2... | collective-permute-start | bytes 1327112 | tf_op jit(solution)/shard_map/while/body/eval_jaxpr/ppermute | solution.py:35
  932.1 75.9 %collective-permute-start.3 = (bf16[576,2,192]{0,2,1:T(8,128)(2,1)S(1)}, bf16[576,2,192]{0,2,1:T(8,128)(2,1)S(1)}, u32[]{:S(2)}, u32[]{:S(2)}) collective-permute-start(bf16[576,2,192]{0,2,1:T(8,128)(2,1)S(1)} %slice.568), channel_id=1, source_target_pairs={{4,0},{8,4},{12,8},{16,12},{20,16},{24,20},{28,24},{5,1},{9,5},{13... | collective-permute-start | bytes 1327112 | tf_op jit(solution)/shard_map/while/body/eval_jaxpr/ppermute | solution.py:35
  933.4 74.6 %collective-permute-start.2 = (bf16[576,2,192]{0,2,1:T(8,128)(2,1)S(1)}, bf16[576,2,192]{0,2,1:T(8,128)(2,1)}, u32[]{:S(2)}, u32[]{:S(2)}) collective-permute-start(bf16[576,2,192]{0,2,1:T(8,128)(2,1)S(1)} %slice.568), channel_id=1, source_target_pairs={{0,4},{4,8},{8,12},{12,16},{16,20},{20,24},{24,28},{1,5},{5,9},{9,... | collective-permute-start | bytes 1327112 | tf_op jit(solution)/shard_map/while/body/eval_jaxpr/ppermute | solution.py:35
  938.8 69.2 %collective-permute-start.1 = (bf16[576,2,192]{0,2,1:T(8,128)(2,1)S(1)}, bf16[576,2,192]{0,2,1:T(8,128)(2,1)}, u32[]{:S(2)}, u32[]{:S(2)}) collective-permute-start(bf16[576,2,192]{0,2,1:T(8,128)(2,1)S(1)} %slice.568), channel_id=1, source_target_pairs={{0,8},{4,12},{8,16},{12,20},{16,24},{20,28},{1,9},{5,13},{9,17},{1... | collective-permute-start | bytes 1327112 | tf_op jit(solution)/shard_map/while/body/eval_jaxpr/ppermute | solution.py:35
  1064.8 50.7 %all-gather.23.cloned.1.call-start = ((), (), s32[]{:S(2)}) async-start(), calls=%async_computation.15 | async-start | bytes 1327104 | tf_op jit(solution)/shard_map/while/body/eval_jaxpr/all_gather | solution.py:58
  1065.6 92.1 %all-gather.25.cloned.1.call-start = ((), (), s32[]{:S(2)}) async-start(), calls=%async_computation.16 | async-start | bytes 1327104 | tf_op jit(solution)/shard_map/while/body/eval_jaxpr/all_gather | solution.py:60
  1066.3 117.1 %reduce-scatter.29.cloned.1.call-start = ((), (), s32[]{:S(2)}) async-start(), calls=%async_computation.17 | async-start | bytes 1105920 | tf_op jit(solution)/shard_map/while/body/eval_jaxpr/reduce_scatter | solution.py:80
  1161.1 65.6 %all-gather.27.cloned.1.call-start = ((), (), s32[]{:S(2)}) async-start(), calls=%async_computation.18 | async-start | bytes 1327104 | tf_op jit(solution)/shard_map/while/body/eval_jaxpr/all_gather | solution.py:60
  1185.2 83.4 %all-gather.29.cloned.1.call-start = ((), (), s32[]{:S(2)}) async-start(), calls=%async_computation.19 | async-start | bytes 1327104 | tf_op jit(solution)/shard_map/while/body/eval_jaxpr/all_gather | solution.py:58
  1185.8 205.7 %reduce-scatter.31.cloned.1.call-start = ((), (), s32[]{:S(2)}) async-start(), calls=%async_computation.20 | async-start | bytes 1105920 | tf_op jit(solution)/shard_map/while/body/eval_jaxpr/reduce_scatter | solution.py:96
  1272.0 290.8 %reduce-scatter.33.cloned.1.call-start = ((), (), s32[]{:S(2)}) async-start(), calls=%async_computation.21 | async-start | bytes 1105920 | tf_op jit(solution)/shard_map/while/body/eval_jaxpr/reduce_scatter | solution.py:96
  1485.0 26.7 collective-permute-start.8
  1494.9 24.0 collective-permute-start.11
  1567.7 292.6 %reduce-scatter.27.cloned.1.call-start = ((), (), s32[]{:S(2)}) async-start(), calls=%async_computation.14 | async-start | bytes 1105920 | tf_op jit(solution)/shard_map/while/body/eval_jaxpr/reduce_scatter | solution.py:80
  1694.6 74.6 %collective-permute-start.5 = (bf16[576,2,192]{0,2,1:T(8,128)(2,1)S(1)}, bf16[576,2,192]{0,2,1:T(8,128)(2,1)S(1)}, u32[]{:S(2)}, u32[]{:S(2)}) collective-permute-start(bf16[576,2,192]{0,2,1:T(8,128)(2,1)S(1)} %slice.568), channel_id=1, source_target_pairs={{12,0},{16,4},{20,8},{24,12},{28,16},{13,1},{17,5},{21,9},{25,13},... | collective-permute-start | bytes 1327112 | tf_op jit(solution)/shard_map/while/body/eval_jaxpr/ppermute | solution.py:35
  1695.9 77.1 %collective-permute-start.4 = (bf16[576,2,192]{0,2,1:T(8,128)(2,1)S(1)}, bf16[576,2,192]{0,2,1:T(8,128)(2,1)S(1)}, u32[]{:S(2)}, u32[]{:S(2)}) collective-permute-start(bf16[576,2,192]{0,2,1:T(8,128)(2,1)S(1)} %slice.568), channel_id=1, source_target_pairs={{8,0},{12,4},{16,8},{20,12},{24,16},{28,20},{9,1},{13,5},{17,9},{2... | collective-permute-start | bytes 1327112 | tf_op jit(solution)/shard_map/while/body/eval_jaxpr/ppermute | solution.py:35
  1697.2 75.9 %collective-permute-start.3 = (bf16[576,2,192]{0,2,1:T(8,128)(2,1)S(1)}, bf16[576,2,192]{0,2,1:T(8,128)(2,1)S(1)}, u32[]{:S(2)}, u32[]{:S(2)}) collective-permute-start(bf16[576,2,192]{0,2,1:T(8,128)(2,1)S(1)} %slice.568), channel_id=1, source_target_pairs={{4,0},{8,4},{12,8},{16,12},{20,16},{24,20},{28,24},{5,1},{9,5},{13... | collective-permute-start | bytes 1327112 | tf_op jit(solution)/shard_map/while/body/eval_jaxpr/ppermute | solution.py:35
  1698.5 74.6 %collective-permute-start.2 = (bf16[576,2,192]{0,2,1:T(8,128)(2,1)S(1)}, bf16[576,2,192]{0,2,1:T(8,128)(2,1)}, u32[]{:S(2)}, u32[]{:S(2)}) collective-permute-start(bf16[576,2,192]{0,2,1:T(8,128)(2,1)S(1)} %slice.568), channel_id=1, source_target_pairs={{0,4},{4,8},{8,12},{12,16},{16,20},{20,24},{24,28},{1,5},{5,9},{9,... | collective-permute-start | bytes 1327112 | tf_op jit(solution)/shard_map/while/body/eval_jaxpr/ppermute | solution.py:35
  1703.9 69.2 %collective-permute-start.1 = (bf16[576,2,192]{0,2,1:T(8,128)(2,1)S(1)}, bf16[576,2,192]{0,2,1:T(8,128)(2,1)}, u32[]{:S(2)}, u32[]{:S(2)}) collective-permute-start(bf16[576,2,192]{0,2,1:T(8,128)(2,1)S(1)} %slice.568), channel_id=1, source_target_pairs={{0,8},{4,12},{8,16},{12,20},{16,24},{20,28},{1,9},{5,13},{9,17},{1... | collective-permute-start | bytes 1327112 | tf_op jit(solution)/shard_map/while/body/eval_jaxpr/ppermute | solution.py:35
  1829.9 50.5 %all-gather.23.cloned.1.call-start = ((), (), s32[]{:S(2)}) async-start(), calls=%async_computation.15 | async-start | bytes 1327104 | tf_op jit(solution)/shard_map/while/body/eval_jaxpr/all_gather | solution.py:58
  1830.4 91.9 %all-gather.25.cloned.1.call-start = ((), (), s32[]{:S(2)}) async-start(), calls=%async_computation.16 | async-start | bytes 1327104 | tf_op jit(solution)/shard_map/while/body/eval_jaxpr/all_gather | solution.py:60
  1831.2 116.9 %reduce-scatter.29.cloned.1.call-start = ((), (), s32[]{:S(2)}) async-start(), calls=%async_computation.17 | async-start | bytes 1105920 | tf_op jit(solution)/shard_map/while/body/eval_jaxpr/reduce_scatter | solution.py:80
  1925.8 65.6 %all-gather.27.cloned.1.call-start = ((), (), s32[]{:S(2)}) async-start(), calls=%async_computation.18 | async-start | bytes 1327104 | tf_op jit(solution)/shard_map/while/body/eval_jaxpr/all_gather | solution.py:60
  1949.9 83.5 %all-gather.29.cloned.1.call-start = ((), (), s32[]{:S(2)}) async-start(), calls=%async_computation.19 | async-start | bytes 1327104 | tf_op jit(solution)/shard_map/while/body/eval_jaxpr/all_gather | solution.py:58
  1950.6 205.7 %reduce-scatter.31.cloned.1.call-start = ((), (), s32[]{:S(2)}) async-start(), calls=%async_computation.20 | async-start | bytes 1105920 | tf_op jit(solution)/shard_map/while/body/eval_jaxpr/reduce_scatter | solution.py:96
  2036.8 290.8 %reduce-scatter.33.cloned.1.call-start = ((), (), s32[]{:S(2)}) async-start(), calls=%async_computation.21 | async-start | bytes 1105920 | tf_op jit(solution)/shard_map/while/body/eval_jaxpr/reduce_scatter | solution.py:96
  2249.8 26.7 collective-permute-start.8
  2259.7 24.0 collective-permute-start.11
  2332.6 292.6 %reduce-scatter.27.cloned.1.call-start = ((), (), s32[]{:S(2)}) async-start(), calls=%async_computation.14 | async-start | bytes 1105920 | tf_op jit(solution)/shard_map/while/body/eval_jaxpr/reduce_scatter | solution.py:80
  2459.4 74.6 %collective-permute-start.5 = (bf16[576,2,192]{0,2,1:T(8,128)(2,1)S(1)}, bf16[576,2,192]{0,2,1:T(8,128)(2,1)S(1)}, u32[]{:S(2)}, u32[]{:S(2)}) collective-permute-start(bf16[576,2,192]{0,2,1:T(8,128)(2,1)S(1)} %slice.568), channel_id=1, source_target_pairs={{12,0},{16,4},{20,8},{24,12},{28,16},{13,1},{17,5},{21,9},{25,13},... | collective-permute-start | bytes 1327112 | tf_op jit(solution)/shard_map/while/body/eval_jaxpr/ppermute | solution.py:35
  2460.7 77.1 %collective-permute-start.4 = (bf16[576,2,192]{0,2,1:T(8,128)(2,1)S(1)}, bf16[576,2,192]{0,2,1:T(8,128)(2,1)S(1)}, u32[]{:S(2)}, u32[]{:S(2)}) collective-permute-start(bf16[576,2,192]{0,2,1:T(8,128)(2,1)S(1)} %slice.568), channel_id=1, source_target_pairs={{8,0},{12,4},{16,8},{20,12},{24,16},{28,20},{9,1},{13,5},{17,9},{2... | collective-permute-start | bytes 1327112 | tf_op jit(solution)/shard_map/while/body/eval_jaxpr/ppermute | solution.py:35
  2462.0 75.9 %collective-permute-start.3 = (bf16[576,2,192]{0,2,1:T(8,128)(2,1)S(1)}, bf16[576,2,192]{0,2,1:T(8,128)(2,1)S(1)}, u32[]{:S(2)}, u32[]{:S(2)}) collective-permute-start(bf16[576,2,192]{0,2,1:T(8,128)(2,1)S(1)} %slice.568), channel_id=1, source_target_pairs={{4,0},{8,4},{12,8},{16,12},{20,16},{24,20},{28,24},{5,1},{9,5},{13... | collective-permute-start | bytes 1327112 | tf_op jit(solution)/shard_map/while/body/eval_jaxpr/ppermute | solution.py:35
  2463.3 74.6 %collective-permute-start.2 = (bf16[576,2,192]{0,2,1:T(8,128)(2,1)S(1)}, bf16[576,2,192]{0,2,1:T(8,128)(2,1)}, u32[]{:S(2)}, u32[]{:S(2)}) collective-permute-start(bf16[576,2,192]{0,2,1:T(8,128)(2,1)S(1)} %slice.568), channel_id=1, source_target_pairs={{0,4},{4,8},{8,12},{12,16},{16,20},{20,24},{24,28},{1,5},{5,9},{9,... | collective-permute-start | bytes 1327112 | tf_op jit(solution)/shard_map/while/body/eval_jaxpr/ppermute | solution.py:35
  2468.7 69.2 %collective-permute-start.1 = (bf16[576,2,192]{0,2,1:T(8,128)(2,1)S(1)}, bf16[576,2,192]{0,2,1:T(8,128)(2,1)}, u32[]{:S(2)}, u32[]{:S(2)}) collective-permute-start(bf16[576,2,192]{0,2,1:T(8,128)(2,1)S(1)} %slice.568), channel_id=1, source_target_pairs={{0,8},{4,12},{8,16},{12,20},{16,24},{20,28},{1,9},{5,13},{9,17},{1... | collective-permute-start | bytes 1327112 | tf_op jit(solution)/shard_map/while/body/eval_jaxpr/ppermute | solution.py:35
  2594.7 50.5 %all-gather.23.cloned.1.call-start = ((), (), s32[]{:S(2)}) async-start(), calls=%async_computation.15 | async-start | bytes 1327104 | tf_op jit(solution)/shard_map/while/body/eval_jaxpr/all_gather | solution.py:58
  2595.3 91.9 %all-gather.25.cloned.1.call-start = ((), (), s32[]{:S(2)}) async-start(), calls=%async_computation.16 | async-start | bytes 1327104 | tf_op jit(solution)/shard_map/while/body/eval_jaxpr/all_gather | solution.py:60
  2596.0 117.0 %reduce-scatter.29.cloned.1.call-start = ((), (), s32[]{:S(2)}) async-start(), calls=%async_computation.17 | async-start | bytes 1105920 | tf_op jit(solution)/shard_map/while/body/eval_jaxpr/reduce_scatter | solution.py:80
  2690.6 65.6 %all-gather.27.cloned.1.call-start = ((), (), s32[]{:S(2)}) async-start(), calls=%async_computation.18 | async-start | bytes 1327104 | tf_op jit(solution)/shard_map/while/body/eval_jaxpr/all_gather | solution.py:60
  2714.7 83.5 %all-gather.29.cloned.1.call-start = ((), (), s32[]{:S(2)}) async-start(), calls=%async_computation.19 | async-start | bytes 1327104 | tf_op jit(solution)/shard_map/while/body/eval_jaxpr/all_gather | solution.py:58
  2715.5 205.7 %reduce-scatter.31.cloned.1.call-start = ((), (), s32[]{:S(2)}) async-start(), calls=%async_computation.20 | async-start | bytes 1105920 | tf_op jit(solution)/shard_map/while/body/eval_jaxpr/reduce_scatter | solution.py:96
  2801.6 290.8 %reduce-scatter.33.cloned.1.call-start = ((), (), s32[]{:S(2)}) async-start(), calls=%async_computation.21 | async-start | bytes 1105920 | tf_op jit(solution)/shard_map/while/body/eval_jaxpr/reduce_scatter | solution.py:96
  3014.7 26.7 collective-permute-start.8
  3099.7 73.3 %reduce-scatter.25.cloned.1.call-start = ((), (), s32[]{:S(2)}) async-start(), calls=%async_computation.13 | async-start | bytes 442368
  3101.4 129.8 %reduce-scatter.23.cloned.1.call-start = ((), (), s32[]{:S(2)}) async-start(), calls=%async_computation.12 | async-start | bytes 884736
  3103.7 200.1 %reduce-scatter.17.cloned.1.call-start = ((), (), s32[]{:S(2)}) async-start(), calls=%async_computation.9 | async-start | bytes 2654208 | tf_op jit(solution)/shard_map/reduce_scatter | solution.py:357
  3106.8 270.1 %reduce-scatter.19.cloned.1.call-start = ((), (), s32[]{:S(2)}) async-start(), calls=%async_computation.10 | async-start | bytes 2654208 | tf_op jit(solution)/shard_map/reduce_scatter | solution.py:360
  3107.4 342.5 %reduce-scatter.21.cloned.1.call-start = ((), (), s32[]{:S(2)}) async-start(), calls=%async_computation.11 | async-start | bytes 2654208 | tf_op jit(solution)/shard_map/reduce_scatter | solution.py:362
  (347 other events, 7189.9 us)
Sparse Core Ops, SparseCore 0:
  302.7 30.4 reduce-scatter.26
  398.5 22.1 reduce-scatter.28
  509.5 22.1 reduce-scatter.30
  756.6 41.1 reduce-scatter.32
  1064.9 30.3 reduce-scatter.26
  1161.2 22.1 reduce-scatter.28
  1272.1 22.1 reduce-scatter.30
  1521.6 41.1 reduce-scatter.32
  1830.0 30.3 reduce-scatter.26
  1925.9 22.1 reduce-scatter.28
  2036.9 22.1 reduce-scatter.30
  2286.4 41.1 reduce-scatter.32
  2594.8 30.3 reduce-scatter.26
  2690.8 22.1 reduce-scatter.28
  2801.8 22.1 reduce-scatter.30
  3051.3 41.1 reduce-scatter.32
  3103.5 62.2 reduce-scatter.24
  3168.9 62.2 reduce-scatter.22
  3235.3 68.5 reduce-scatter.16
  3307.8 69.0 reduce-scatter.18
  3380.9 68.8 reduce-scatter.20
Sparse Core Ops, SparseCore 1:
  305.3 47.8 all-gather.22
  355.2 39.7 all-gather.24
  422.6 41.4 all-gather.26
  466.2 39.7 all-gather.28
  1067.8 47.7 all-gather.22
  1117.7 39.9 all-gather.24
  1185.3 41.4 all-gather.26
  1228.8 39.7 all-gather.28
  1832.5 47.8 all-gather.22
  1882.6 39.7 all-gather.24
  1950.0 41.4 all-gather.26
  1993.6 39.7 all-gather.28
  2597.4 47.8 all-gather.22
  2647.4 39.7 all-gather.24
  2714.8 41.4 all-gather.26
  2758.5 39.7 all-gather.28
